TPU v7x, 32 devices: a whole 2x2x4 slice. The times are simulated.
32 devices in a mesh: dp: 8 (over z, y), tensor: 4 (over x, core).
Axes of the slice: x: 2, y: 2, z: 4, core: 2. Of those that a mesh axis runs over, the one named last changes fastest.
Arguments:
- tokens: bfloat16 [8192, 1024], P(('dp', 'tensor')), may hold values from -16 to 16
- cotangent: bfloat16 [8192, 1024], P(('dp', 'tensor')), may hold values from -16 to 16
- gain_attn: float32 [1024], replicated, may hold values from 0.1 to 1.9
- bias_attn: float32 [1024], replicated, may hold values from -1.75 to 1.75
- gain_mlp: float32 [1024], replicated, may hold values from 0.1 to 1.9
- bias_mlp: float32 [1024], replicated, may hold values from -1.75 to 1.75
- qkv_weight: bfloat16 [1024, 3072], P(None, 'tensor'), may hold values from -0.1875 to 0.1875
- qkv_bias: float32 [3072], P('tensor'), may hold values from -1.75 to 1.75
- out_weight: bfloat16 [1024, 1024], P('tensor'), may hold values from -2.5 to 2.5
- out_bias: float32 [1024], replicated, may hold values from -1.75 to 1.75
- up_weight: bfloat16 [1024, 4096], P(None, 'tensor'), may hold values from -0.1875 to 0.1875
- up_bias: float32 [4096], P('tensor'), may hold values from -1.75 to 1.75
- down_weight: bfloat16 [4096, 1024], P('tensor'), may hold values from -0.09375 to 0.09375
- down_bias: float32 [1024], replicated, may hold values from -1.75 to 1.75
Outputs:
- mixed: bfloat16 [8192, 1024], P(('dp', 'tensor'))
- input_grad: float32 [8192, 1024], P(('dp', 'tensor'))
- gain_attn_grad: float32 [1024], replicated
- bias_attn_grad: float32 [1024], replicated
- gain_mlp_grad: float32 [1024], replicated
- bias_mlp_grad: float32 [1024], replicated
- qkv_weight_grad: float32 [1024, 3072], P(None, 'tensor')
- qkv_bias_grad: float32 [3072], P('tensor')
- out_weight_grad: float32 [1024, 1024], P('tensor')
- out_bias_grad: float32 [1024], replicated
- up_weight_grad: float32 [1024, 4096], P(None, 'tensor')
- up_bias_grad: float32 [4096], P('tensor')
- down_weight_grad: float32 [4096, 1024], P('tensor')
- down_bias_grad: float32 [1024], replicated
- statistics: float32 [3], replicated
All inputs are finite; a program needn't handle non-finite values.
Results may differ from a plain program's by a relative error of at most 0.012.
The roundings to bfloat16 on the way count: a program that leaves them out, or rounds other values in their place, can miss the bound.
Values may be sent and summed in bfloat16 or wider, within the bound.
A program may use at most 192 MiB of HBM per device.

v0:
```python
import math

import jax
import jax.numpy as jnp
from jax import lax
from jax.sharding import PartitionSpec as P

HD = 64
ROT = 16


epsilon = 1e-05


def angle_tables(seq_len):
    positions = jnp.arange(seq_len, dtype=jnp.float32)
    inverse = 10000.0 ** (-(jnp.arange(ROT // 2, dtype=jnp.float32) * 2.0 / ROT))
    angles = positions[:, None] * inverse[None, :]
    cosine = jnp.concatenate([jnp.cos(angles), jnp.cos(angles)], axis=-1)[:, None, :]
    sine_part = jnp.concatenate([jnp.sin(angles), jnp.sin(angles)], axis=-1)[:, None, :]
    return (cosine, sine_part)


def rotate(field_in, cosine, sine_part):
    half_rot = ROT // 2
    first_half = field_in[..., :half_rot]
    second = field_in[..., half_rot:ROT]
    turned = jnp.concatenate([-second, first_half], axis=-1)
    return jnp.concatenate(
        [field_in[..., :ROT] * cosine + turned * sine_part, field_in[..., ROT:]], axis=-1
    )


def unrotate(grad_in, cosine, sine_part):
    half_rot = ROT // 2
    head_part = grad_in[..., :ROT]
    scaled = head_part * sine_part
    turned = jnp.concatenate([scaled[..., half_rot:], -scaled[..., :half_rot]], axis=-1)
    return jnp.concatenate([head_part * cosine + turned, grad_in[..., ROT:]], axis=-1)


def normalize(raw_rows):
    average = jnp.mean(raw_rows, axis=-1, keepdims=True)
    centred = raw_rows - average
    spread = jnp.mean(centred * centred, axis=-1, keepdims=True)
    inverse_root = lax.rsqrt(spread + epsilon)
    return (centred * inverse_root, inverse_root)


def against(left, right):
    return lax.dot_general(
        left, right, (((1,), (1,)), ((), ())), preferred_element_type=jnp.float32
    )


def per_device(
    tokens,
    cotangent,
    gain_attn,
    bias_attn,
    gain_mlp,
    bias_mlp,
    qkv_weight,
    qkv_bias,
    out_weight,
    out_bias,
    up_weight,
    up_bias,
    down_weight,
    down_bias,
):
    own_rows = tokens.shape[0]
    model_width = tokens.shape[1]
    heads_here = out_weight.shape[0] // HD
    score_scale = HD ** (-0.5)
    whole_rows = lax.all_gather(tokens, "tensor", axis=0, tiled=True)
    seq_len = whole_rows.shape[0]
    normed, _ = normalize(whole_rows.astype(jnp.float32))
    attention_input = (normed * gain_attn + bias_attn).astype(jnp.bfloat16)
    feed_input = (normed * gain_mlp + bias_mlp).astype(jnp.bfloat16)
    projected = jnp.dot(attention_input, qkv_weight, preferred_element_type=jnp.float32) + qkv_bias
    projected = projected.reshape(seq_len, heads_here, 3, HD)
    cosine, sine_part = angle_tables(seq_len)
    queries = rotate(projected[:, :, 0], cosine, sine_part).astype(jnp.bfloat16)
    keys_all = rotate(projected[:, :, 1], cosine, sine_part).astype(jnp.bfloat16)
    values_all = projected[:, :, 2].astype(jnp.bfloat16)
    preact = jnp.dot(feed_input, up_weight, preferred_element_type=jnp.float32) + up_bias
    hidden = jax.nn.gelu(preact, approximate=False).astype(jnp.bfloat16)
    block_rows = min(512, seq_len)
    block_total = seq_len // block_rows
    key_positions = jnp.arange(seq_len, dtype=jnp.int32)

    def causal_mask(offset):
        return key_positions[None, :] <= (offset + jnp.arange(block_rows, dtype=jnp.int32))[:, None]

    def forward_block(number):
        offset = number * block_rows
        query_rows = lax.dynamic_slice_in_dim(queries, offset, block_rows, 0)
        scores = (
            jnp.einsum("qhd,khd->hqk", query_rows, keys_all, preferred_element_type=jnp.float32)
            * score_scale
        )
        scores = jnp.where(causal_mask(offset)[None], scores, -1e30)
        highest = jnp.max(scores, axis=-1, keepdims=True)
        weights = jnp.exp(scores - highest)
        totals = jnp.sum(weights, axis=-1, keepdims=True)
        soft_rows = (weights / totals).astype(jnp.bfloat16)
        context_rows = jnp.einsum(
            "hqk,khd->qhd", soft_rows, values_all, preferred_element_type=jnp.float32
        ).astype(jnp.bfloat16)
        log_totals = (highest + jnp.log(totals))[:, :, 0].T
        return (context_rows, log_totals)

    context_blocks, log_blocks = lax.map(forward_block, jnp.arange(block_total, dtype=jnp.int32))
    context = context_blocks.reshape(seq_len, heads_here * HD)
    log_sums = log_blocks.reshape(seq_len, heads_here)
    context_rows = context
    branch = lax.psum_scatter(
        jnp.dot(context_rows, out_weight, preferred_element_type=jnp.float32)
        + jnp.dot(hidden, down_weight, preferred_element_type=jnp.float32),
        "tensor",
        scatter_dimension=0,
        tiled=True,
    )
    branch = branch + out_bias + down_bias
    residual_out = tokens.astype(jnp.float32) + branch
    mixed_out = residual_out.astype(jnp.bfloat16)
    forward_squares = jnp.stack([jnp.sum(residual_out * residual_out), jnp.sum(branch * branch)])
    forward_totals = lax.psum(forward_squares, ("dp", "tensor"))
    upstream = lax.all_gather(cotangent, "tensor", axis=0, tiled=True)
    out_weight_grad = jnp.einsum("sa,sd->ad", context, upstream, preferred_element_type=jnp.float32)
    down_weight_grad = jnp.einsum("sf,sd->fd", hidden, upstream, preferred_element_type=jnp.float32)
    context_grad = against(upstream, out_weight).astype(jnp.bfloat16)
    hidden_grad = against(upstream, down_weight)
    normal_cdf = 0.5 * (1.0 + lax.erf(preact * 0.5**0.5))
    density = jnp.exp(-0.5 * preact * preact) * (1.0 / math.sqrt(2.0 * math.pi))
    preact_grad = (hidden_grad * (normal_cdf + preact * density)).astype(jnp.bfloat16)
    context_grad3 = context_grad.reshape(seq_len, heads_here, HD)

    def backward_block(carried, number):
        key_grad, value_grad = carried
        offset = number * block_rows
        query_rows = lax.dynamic_slice_in_dim(queries, offset, block_rows, 0)
        grad_rows = lax.dynamic_slice_in_dim(context_grad3, offset, block_rows, 0)
        log_rows = lax.dynamic_slice_in_dim(log_sums, offset, block_rows, 0).T
        scores = (
            jnp.einsum("qhd,khd->hqk", query_rows, keys_all, preferred_element_type=jnp.float32)
            * score_scale
        )
        soft_full = jnp.exp(
            jnp.where(causal_mask(offset)[None], scores - log_rows[:, :, None], -1e30)
        )
        prob_grad = jnp.einsum(
            "qhd,khd->hqk", grad_rows, values_all, preferred_element_type=jnp.float32
        )
        deltas = jnp.sum(soft_full * prob_grad, axis=-1, keepdims=True)
        score_grad = (soft_full * (prob_grad - deltas)).astype(jnp.bfloat16)
        query_grad = (
            jnp.einsum("hqk,khd->qhd", score_grad, keys_all, preferred_element_type=jnp.float32)
            * score_scale
        )
        key_grad = (
            key_grad
            + jnp.einsum("hqk,qhd->khd", score_grad, query_rows, preferred_element_type=jnp.float32)
            * score_scale
        )
        value_grad = value_grad + jnp.einsum(
            "hqk,qhd->khd",
            soft_full.astype(jnp.bfloat16),
            grad_rows,
            preferred_element_type=jnp.float32,
        )
        return ((key_grad, value_grad), query_grad)

    empty = jnp.zeros((seq_len, heads_here, HD), jnp.float32)
    (key_grad, value_grad), query_blocks = lax.scan(
        backward_block, (empty, empty), jnp.arange(block_total, dtype=jnp.int32)
    )
    query_grad = unrotate(query_blocks.reshape(seq_len, heads_here, HD), cosine, sine_part)
    key_grad = unrotate(key_grad, cosine, sine_part)
    qkv_grad = (
        jnp.stack([query_grad, key_grad, value_grad], axis=2)
        .reshape(seq_len, 3 * heads_here * HD)
        .astype(jnp.bfloat16)
    )
    qkv_weight_grad = jnp.einsum(
        "sd,sc->dc", attention_input, qkv_grad, preferred_element_type=jnp.float32
    )
    qkv_bias_grad = jnp.sum(qkv_grad, axis=0, dtype=jnp.float32)
    up_weight_grad = jnp.einsum(
        "sd,sf->df", feed_input, preact_grad, preferred_element_type=jnp.float32
    )
    up_bias_grad = jnp.sum(preact_grad, axis=0, dtype=jnp.float32)
    own_normed, own_scale = normalize(tokens.astype(jnp.float32))
    attention_back = against(qkv_grad, qkv_weight)
    feed_back = against(preact_grad, up_weight)
    gain_terms = jnp.stack(
        [
            jnp.sum(normed * attention_back, axis=0),
            jnp.sum(attention_back, axis=0),
            jnp.sum(normed * feed_back, axis=0),
            jnp.sum(feed_back, axis=0),
        ]
    )
    normed_grad = lax.psum_scatter(
        (attention_back * gain_attn + feed_back * gain_mlp).astype(jnp.bfloat16),
        "tensor",
        scatter_dimension=0,
        tiled=True,
    ).astype(jnp.float32)
    centred_term = (
        normed_grad
        - jnp.mean(normed_grad, axis=-1, keepdims=True)
        - own_normed * jnp.mean(normed_grad * own_normed, axis=-1, keepdims=True)
    )
    input_grad = own_scale * centred_term + cotangent.astype(jnp.float32)
    (
        qkv_weight_grad,
        qkv_bias_grad,
        out_weight_grad,
        up_weight_grad,
        up_bias_grad,
        down_weight_grad,
    ) = lax.psum(
        (
            qkv_weight_grad,
            qkv_bias_grad,
            out_weight_grad,
            up_weight_grad,
            up_bias_grad,
            down_weight_grad,
        ),
        "dp",
    )
    bias_rows = jnp.sum(cotangent, axis=0, dtype=jnp.float32)
    grad_square = jnp.sum(input_grad * input_grad)
    gain_totals, bias_totals, grad_total = lax.psum(
        (gain_terms, bias_rows, grad_square), ("dp", "tensor")
    )
    square_totals = jnp.concatenate([forward_totals, grad_total[None]])
    elements = own_rows * model_width * lax.axis_size("dp") * lax.axis_size("tensor")
    statistics = jnp.sqrt(square_totals / elements)
    return (
        mixed_out,
        input_grad,
        gain_totals[0],
        gain_totals[1],
        gain_totals[2],
        gain_totals[3],
        qkv_weight_grad,
        qkv_bias_grad,
        out_weight_grad,
        bias_totals,
        up_weight_grad,
        up_bias_grad,
        down_weight_grad,
        bias_totals,
        statistics,
    )


def solution(mesh):
    in_specs = (
        P(("dp", "tensor"), None),
        P(("dp", "tensor"), None),
        P(),
        P(),
        P(),
        P(),
        P(None, "tensor"),
        P("tensor"),
        P("tensor", None),
        P(),
        P(None, "tensor"),
        P("tensor"),
        P("tensor", None),
        P(),
    )
    out_specs = (
        P(("dp", "tensor"), None),
        P(("dp", "tensor"), None),
        P(),
        P(),
        P(),
        P(),
        P(None, "tensor"),
        P("tensor"),
        P("tensor", None),
        P(),
        P(None, "tensor"),
        P("tensor"),
        P("tensor", None),
        P(),
        P(),
    )
    return jax.shard_map(
        per_device, mesh=mesh, in_specs=in_specs, out_specs=out_specs, check_vma=False
    )
```

profile of v0, /device:TPU:0, one launch (start us, length us, event | category | flops | bytes accessed | tf_op | source)
XLA Modules:
  0.0 678.1 jit_solution(6702302602257500573)
XLA Ops:
  9.1 25.9 %all-gather.3.cloned.1.call-done = bf16[1024,1024]{1,0:T(8,128)(2,1)} async-done(((bf16[256,1024]{1,0:T(8,128)(2,1)}), bf16[1024,1024]{1,0:T(8,128)(2,1)}) %all-gather.3.cloned.1.call-update) | async-done | bytes 2097168 | tf_op jit(solution)/shard_map/all_gather | solution.py:76
  44.1 21.8 %while.28 = (s32[]{:T(128)}, bf16[2,512,4,64]{1,3,2,0:T(8,128)(2,1)}, f32[2,512,4]{1,2,0:T(4,128)S(1)}, s32[2]{0:T(128)S(1)}, bf16[1024,4,64]{0,2,1:T(8,128)(2,1...) while((s32[]{:T(128)}, ...), condition=%wide.region_5.6_spmd.clone, body=%wide.region_2.5_spmd.clone.sunk | while | flops 562690560 | bytes 28906164 | solution.py:114
  45.7 2.6 fusion.148
  50.7 4.3 fusion.150
  61.7 4.3 fusion.150
  66.0 3.1 convolution_convert_fusion
  69.1 71.8 %while.29 = (s32[]{:T(128)}, f32[1024,4,64]{0,2,1:T(8,128)}, f32[1024,4,64]{0,2,1:T(8,128)}, f32[2,512,4,64]{1,0,3,2:T(2,128)}, s32[2]{0:T(128)S(1)}, /*index=5*...) while((s32[]{:T(128)}, f32[1024,4,64]{0,2,1:T(8,128)}, ...), condition=%wide.region_11.12_spmd.clone, body=%wide.region_9.11_spmd.clone.sunk | while | flops 1375599104 | bytes 162591104 | solution.py:176
  73.2 4.7 multiply_reduce_fusion.5
  85.2 10.4 %dynamic_update_slice.22 = f32[2,512,4,64]{1,0,3,2:T(2,128)} dynamic-update-slice(f32[2,512,4,64]{1,0,3,2:T(2,128)} %get-tuple-element.430, f32[1,512,4,64]{1,0,3,2:T(1,128)} %copy.73, s32[]{:T(128)} %get-tuple-element.427, s32[]{:T(128)} %constant.73.clone.1..sunk.1, s32[]{:T(128)} %constant.73.clone.1..sunk.1, s32[]{:T(128)} %constant.73.clone.1..sunk.1) | dynamic-update-slice | bytes 1048580 | tf_op jit(solution)/shard_map/while/body/jit(dynamic_update_index_in_dim)/dynamic_update_slice | solution.py:176
  95.6 4.2 fusion.161
  100.8 3.7 fusion.162
  108.4 4.7 multiply_reduce_fusion.5
  120.4 10.4 %dynamic_update_slice.22 = f32[2,512,4,64]{1,0,3,2:T(2,128)} dynamic-update-slice(f32[2,512,4,64]{1,0,3,2:T(2,128)} %get-tuple-element.430, f32[1,512,4,64]{1,0,3,2:T(1,128)} %copy.73, s32[]{:T(128)} %get-tuple-element.427, s32[]{:T(128)} %constant.73.clone.1..sunk.1, s32[]{:T(128)} %constant.73.clone.1..sunk.1, s32[]{:T(128)} %constant.73.clone.1..sunk.1) | dynamic-update-slice | bytes 1048580 | tf_op jit(solution)/shard_map/while/body/jit(dynamic_update_index_in_dim)/dynamic_update_slice | solution.py:176
  130.8 4.5 fusion.161
  136.2 4.7 fusion.162
  140.9 3.2 reshape.177
  149.4 13.1 %fusion.55 = (bf16[1024,1024]{1,0:T(8,128)(2,1)}, f32[1024,1024]{1,0:T(8,128)S(1)}) fusion(f32[1024]{0:T(1024)S(1)} %copy-done.36, bf16[1024,1024]{1,0:T(8,128)(2,1)S(1)} %copy-done, bf16[1024,1024]{1,0:T(8,128)(2,1)S(1)} %copy-done.7, f32[1024]{0:T(1024)S(1)} %copy-done.41, f32[1024]{0:T(1024)S(1)} %copy-done.42, f32[1024]{0:T(1024)S(1)} %copy-done.30, ...), kind=kOutput, calls=%fused_computation.66 | convolution fusion | flops 2222981120 | bytes 10506240 | tf_op jit(solution)/shard_map/dot_general | solution.py:87
  162.5 3.9 convert_reduce_fusion.1
  168.9 4.4 fusion.50
  175.0 4.6 fusion.96
  179.7 2.8 convolution_add_fusion
  182.8 3.3 fusion.98
  186.1 6.1 fusion.89
  192.2 4.4 fusion.99
  196.6 4.8 fusion.85
  202.9 22.2 %all-reduce.1 = (f32[768]{0:T(1024)}, f32[1024]{0:T(1024)}) all-reduce(f32[768]{0:T(1024)S(1)} %reduce_sum.175, f32[1024]{0:T(1024)S(1)} %get-tuple-element.262), channel_id=1, replica_groups=mesh['dp'=8,'tensor'=4] {'dp'}, use_global_device_ids=true, to_apply=%region_22.23 | all-reduce | flops 1792 | bytes 14336 | tf_op jit(solution)/shard_map/psum | solution.py:224
  225.2 27.4 %reduce-scatter.3.cloned.1.call-done = f32[256,1024]{1,0:T(8,128)} async-done(((f32[1024,1024]{1,0:T(8,128)}), f32[256,1024]{1,0:T(8,128)}) %reduce-scatter.3.cloned.1.call-update) | async-done | bytes 1048592 | tf_op jit(solution)/shard_map/reduce_scatter | solution.py:118
  252.6 3.4 multiply_reduce_fusion.3
  257.4 3.1 multiply_reduce_fusion.1
  260.5 42.6 %all-reduce = (f32[4,1024]{1,0:T(4,128)S(1)}, f32[1024]{0:T(1024)S(1)}, f32[1]{0:T(128)}, f32[2]{0:T(128)S(1)}) all-reduce(f32[4,1024]{1,0:T(4,128)S(1)} %pad_maximum_fusion.4, f32[1024]{0:T(1024)S(1)} %get-tuple-element.243, f32[1]{0:T(128)} %bitcast.20, f32[2]{0:T(128)S(1)} %pad_maximum_fusion.5), channel_id=1, replica_groups=mesh['dp'=8,'tensor'=4] {'dp','tensor'}, use_global_device_ids=true, to_apply=%region_19.20 | all-reduce | flops 5123 | bytes 40984 | tf_op jit(solution)/shard_map/psum | solution.py:237
  304.9 355.0 %all-reduce.5.cloned.1.call-done = (f32[1024,768]{1,0:T(8,128)}, f32[256,1024]{1,0:T(8,128)}, f32[1024,1024]{1,0:T(8,128)}, f32[1024,1024]{1,0:T(8,128)}) async-done(((f32[1024,768]{1,0:T(8,128)}, f32[256,1024]{1,0:T(8,128)}, f32[1024,1024]{1,0:T(8,128)}, f32[1024,1024]{1,0:T(8,128)}), (f32[1024,768]{1,0:T(8,128)}, f32[256,1024]{1,0:T(8,128)}, f32[1024,1024]{1,0:T(8,128)}, ...) | async-done | bytes 12582928 | tf_op jit(solution)/shard_map/psum | solution.py:224
  660.6 3.9 copy.104
  (195 shorter events, 64.4 us)
Async XLA Ops:
  7.2 141.1 %copy-start = (bf16[1024,1024]{1,0:T(8,128)(2,1)S(1)}, bf16[1024,1024]{1,0:T(8,128)(2,1)}, u32[]{:S(2)}) copy-start(bf16[1024,1024]{1,0:T(8,128)(2,1)} %param.28) | copy-start | bytes 6291460
  7.2 32.1 %copy-start.37 = (f32[1024]{0:T(1024)S(1)}, f32[1024]{0:T(1024)}, u32[]{:S(2)}) copy-start(f32[1024]{0:T(1024)} %param.20) | copy-start | bytes 12292
  7.2 32.1 %copy-start.39 = (f32[1024]{0:T(1024)S(1)}, f32[1024]{0:T(1024)}, u32[]{:S(2)}) copy-start(f32[1024]{0:T(1024)} %param.21) | copy-start | bytes 12292
  7.2 32.1 %copy-start.35 = (f32[768]{0:T(1024)S(1)}, f32[768]{0:T(1024)}, u32[]{:S(2)}) copy-start(f32[768]{0:T(1024)} %param.25) | copy-start | bytes 9220
  7.2 27.7 %all-gather.3.cloned.1.call-start = ((), (), s32[]{:S(2)}) async-start(), calls=%async_computation.2 | async-start | bytes 2621440 | tf_op jit(solution)/shard_map/all_gather | solution.py:76
  8.0 58.0 %all-gather.5.cloned.1.call-start = ((), (), s32[]{:S(2)}) async-start(), calls=%async_computation.4 | async-start | bytes 2621440 | tf_op jit(solution)/shard_map/all_gather | solution.py:130
  8.7 216.5 %reduce-scatter.5.cloned.1.call-start = ((), (), s32[]{:S(2)}) async-start(), calls=%async_computation.5 | async-start | bytes 2621440 | tf_op jit(solution)/shard_map/reduce_scatter | solution.py:205
  9.0 34.1 %copy-start.19 = (f32[1024,16]{0,1:T(8,128)}, f32[1024,16]{0,1:T(8,128)S(1)}, u32[]{:S(2)}) copy-start(f32[1024,16]{0,1:T(8,128)S(1)} %get-tuple-element.267) | copy-start | bytes 196612
  9.1 34.1 %copy-start.21 = (f32[1024,16]{0,1:T(8,128)}, f32[1024,16]{0,1:T(8,128)S(1)}, u32[]{:S(2)}) copy-start(f32[1024,16]{0,1:T(8,128)S(1)} %get-tuple-element.266) | copy-start | bytes 196612
  44.1 21.9 %copy-start.23 = (bf16[256,1024]{1,0:T(8,128)(2,1)S(1)}, bf16[256,1024]{1,0:T(8,128)(2,1)}, u32[]{:S(2)}) copy-start(bf16[256,1024]{1,0:T(8,128)(2,1)} %param.26) | copy-start | bytes 1572868
  69.1 76.3 %copy-start.20 = (f32[1024,16]{0,1:T(8,128)S(1)}, f32[1024,16]{0,1:T(8,128)}, u32[]{:S(2)}) copy-start(f32[1024,16]{0,1:T(8,128)} %copy-done.19) | copy-start | bytes 196612
  72.8 5.2 copy-start.1
  95.6 5.1 copy-start.2
  95.6 5.1 copy-start.12
  108.0 5.1 copy-start.1
  130.8 5.4 copy-start.2
  130.8 5.5 copy-start.12
  140.9 5.6 copy-start.4
  140.9 5.7 copy-start.22
  149.3 19.5 %copy-start.16 = (bf16[1024,4,3,64]{0,3,2,1:T(8,128)(2,1)}, bf16[1024,4,3,64]{0,3,2,1:T(8,128)(2,1)S(1)}, u32[]{:S(2)}) copy-start(bf16[1024,4,3,64]{0,3,2,1:T(8,128)(2,1)S(1)} %copy.43) | copy-start | bytes 4718596
  149.4 13.1 %copy-start.13 = (bf16[1024,1024]{1,0:T(8,128)(2,1)S(1)}, bf16[1024,1024]{1,0:T(8,128)(2,1)}, u32[]{:S(2)}) copy-start(bf16[1024,1024]{1,0:T(8,128)(2,1)} %all-gather.5.cloned.1.call-done) | copy-start | bytes 6291460
  149.4 13.1 %copy-start.32 = (bf16[1024,1024]{1,0:T(8,128)(2,1)S(1)}, bf16[1024,1024]{1,0:T(8,128)(2,1)}, u32[]{:S(2)}) copy-start(bf16[1024,1024]{1,0:T(8,128)(2,1)} %param.30) | copy-start | bytes 6291460
  173.3 79.3 %reduce-scatter.3.cloned.1.call-start = ((), (), s32[]{:S(2)}) async-start(), calls=%async_computation.3 | async-start | bytes 5242880 | tf_op jit(solution)/shard_map/reduce_scatter | solution.py:118
  175.0 4.6 copy-start.24
  182.5 477.5 %all-reduce.5.cloned.1.call-start = ((), (), s32[]{:S(2)}) async-start(), calls=%async_computation.6 | async-start | bytes 25165824 | tf_op jit(solution)/shard_map/psum | solution.py:224
  186.1 6.1 copy-start.14
  186.1 6.1 copy-start.45
  201.4 51.2 %copy-start.27 = (f32[1024]{0:T(1024)S(1)}, f32[1024]{0:T(1024)}, u32[]{:S(2)}) copy-start(f32[1024]{0:T(1024)} %param.31) | copy-start | bytes 12292
  201.4 51.2 %copy-start.28 = (f32[1024]{0:T(1024)S(1)}, f32[1024]{0:T(1024)}, u32[]{:S(2)}) copy-start(f32[1024]{0:T(1024)} %param.27) | copy-start | bytes 12292
  201.4 56.0 %copy-start.15 = (bf16[256,1024]{1,0:T(8,128)(2,1)S(1)}, bf16[256,1024]{1,0:T(8,128)(2,1)}, u32[]{:S(2)}) copy-start(bf16[256,1024]{1,0:T(8,128)(2,1)} %param.19) | copy-start | bytes 1572868
  303.1 362.4 %copy-start.31 = (f32[1024]{0:T(1024)}, f32[1024]{0:T(1024)S(1)}, u32[]{:S(2)}) copy-start(f32[1024]{0:T(1024)S(1)} %get-tuple-element.494) | copy-start | bytes 12292
  660.5 4.9 copy-start.10
  (24 other events, 67.3 us)
Sparse Core Ops, SparseCore 0:
  9.6 25.2 all-gather.2
  36.5 22.5 all-gather.4
  173.4 31.4 reduce-scatter.4
  208.0 44.5 reduce-scatter.2
  258.3 401.5 all-reduce.4
where the time goes:
time: 687 us; the launch traced here: 678 us
  waiting for transfers between devices  410 us (60%)
  matrix products  103 us (15%)
  blocking collectives  64.7 us (9%)
  local copies, waits for them, and re-layouts  53.5 us (8%)
  other arithmetic  28.8 us (4%)
  between operations  14.8 us (2%)
    psum x1, waiting for transfers between devices, per_device(): lax.psum((qkv_weight_grad, qkv_bias_grad, out_weight_grad, up_weight_grad...  355 us
    psum x1, blocking collectives, per_device(): lax.psum((gain_terms, bias_rows, grad_square), ('dp', 'tensor'))  42.6 us
    reduce_scatter x1, waiting for transfers between devices, per_device(): lax.psum_scatter(jnp.dot(context_rows, out_weight, preferred_element_type...  27.4 us
    all_gather x1, waiting for transfers between devices, per_device(): whole_rows = lax.all_gather(tokens, 'tensor', axis=0, tiled=True)  25.9 us
    dynamic_update_slice x4, local copies, waits for them, and re-layouts, per_device(): lax.scan(backward_block, (empty, empty), jnp.arange(block_total, dtype=jn...  23.5 us
    psum x1, blocking collectives, per_device(): lax.psum((qkv_weight_grad, qkv_bias_grad, out_weight_grad, up_weight_grad...  22.2 us
    dot_general x4, matrix products, against(): lax.dot_general(left, right, (((1,), (1,)), ((), ())), preferred_element_...  13.9 us
  transfers between devices with their start and end apart: 5, of which 3 were waited for; matrix products, arithmetic and copies ran while one was open for 10% of the time, Pallas kernels for 0%

commit v1 on v0

--- a/solution.py
+++ b/solution.py
@@ -1,12 +1,17 @@
+import functools
 import math
 
 import jax
 import jax.numpy as jnp
+import numpy as np
 from jax import lax
+from jax.experimental import pallas as pl
+from jax.experimental.pallas import tpu as pltpu
 from jax.sharding import PartitionSpec as P
 
 HD = 64
 ROT = 16
+VMEM_LIMIT = 62 << 20
 
 
 epsilon = 1e-05
@@ -259,6 +264,686 @@
     )
 
 
+F32 = jnp.float32
+BF16 = jnp.bfloat16
+MESH = pl.DeviceIdType.MESH
+TILE = 256
+RING_X = 4
+
+
+def dot_nn(left, right):
+    return jnp.dot(left, right, preferred_element_type=F32)
+
+
+def dot_nt(left, right):
+    return lax.dot_general(left, right, (((1,), (1,)), ((), ())), preferred_element_type=F32)
+
+
+def dot_tn(left, right):
+    return lax.dot_general(left, right, (((0,), (0,)), ((), ())), preferred_element_type=F32)
+
+
+def fused_kernel(
+    ring,
+    tok, cot, ga, ba, gm, bm, bo, bd, bqkv, bup, wqkv_h, wout_h, wup_h, wdn_h, cos_a, sin_a, cos_b, sin_b,
+    mixed, igrad, gd_o, gu_o, gq_o, go_o, sv_o,
+    T, C, AI, FI, HID, GP, PG, QG, QH, KH, VH, CGH, CTXH, CTX, DQ, DKT, DVT, SCO, DPS, COS, SIN,
+    WQKV, WOUT, WUP, WDN, RSB, GB, PSC, PART, RA, RB, SV, ES, EX,
+    lsem, g_s, g_r, r_s, r_r, b_s, b_r, e_s, e_r, o_s, p_s,
+):
+    rows = tok.shape[0]
+    width = tok.shape[1]
+    seq = T.shape[0]
+    heads = QH.shape[0]
+    hidden_width = WUP.shape[1]
+    half_rows = rows // 2
+    blocks = seq // TILE
+    scale = HD ** (-0.5)
+    dp = lax.axis_index("dp")
+    t = lax.axis_index("tensor")
+    core = lax.rem(t, 2)
+    x = lax.div(t, 2)
+    depth = ring // 2
+    y = lax.rem(dp, 2)
+    z = lax.div(dp, 2)
+    at = z + y * (2 * depth - 1 - 2 * z)
+
+    def ring_device(place):
+        ny = lax.div(place, depth)
+        return (2 * (place + ny * (2 * depth - 1 - 2 * place)) + ny, t)
+
+    following = ring_device(lax.rem(at + 1, ring))
+    previous = ring_device(lax.rem(at + ring - 1, ring))
+    onward = (following, previous)
+    core_mate = (dp, t + 1 - 2 * core)
+    x_block = 2 * (1 - x) + core
+    x_mate = (dp, x_block)
+
+    def remote(src, dst, send, recv, device):
+        return pltpu.make_async_remote_copy(
+            src_ref=src, dst_ref=dst, send_sem=send, recv_sem=recv, device_id=device, device_id_type=MESH
+        )
+
+    def gather(which, kind):
+        src, full = (tok, T) if which == 0 else (cot, C)
+        sems = (g_s.at[which, kind], g_r.at[which, kind])
+        if kind == 0:
+            return remote(src, full.at[pl.ds(t * rows, rows)], *sems, core_mate)
+        if kind <= 2:
+            off = (kind - 1) * half_rows
+            return remote(
+                src.at[pl.ds(off, half_rows)], full.at[pl.ds(t * rows + off, half_rows)], *sems, x_mate
+            )
+        part = full.at[pl.ds(x_block * rows + (kind - 3) * half_rows, half_rows)]
+        return remote(part, part, *sems, core_mate)
+
+    local = [
+        pltpu.make_async_copy(tok, T.at[pl.ds(t * rows, rows)], lsem.at[0]),
+        pltpu.make_async_copy(cot, C.at[pl.ds(t * rows, rows)], lsem.at[1]),
+        pltpu.make_async_copy(wqkv_h, WQKV, lsem.at[2]),
+        pltpu.make_async_copy(wup_h, WUP, lsem.at[3]),
+        pltpu.make_async_copy(wdn_h, WDN, lsem.at[4]),
+        pltpu.make_async_copy(wout_h, WOUT, lsem.at[5]),
+    ]
+    gather(0, 1).start()
+    gather(0, 2).start()
+    gather(0, 0).start()
+    for copy in (local[0], local[2], local[3], local[1], local[4], local[5]):
+        copy.start()
+
+    @pl.loop(0, seq // 32)
+    def _(a):
+        ca, sa = cos_a[pl.ds(a, 1), :], sin_a[pl.ds(a, 1), :]
+        cb, sb = cos_b[...], sin_b[...]
+        COS[pl.ds(a * 32, 32), :] = ca * cb - sa * sb
+        SIN[pl.ds(a * 32, 32), :] = sa * cb + ca * sb
+
+    SV[...] = jnp.zeros_like(SV)
+
+    @pl.loop(0, heads)
+    def _(h):
+        DKT[h] = jnp.zeros(DKT.shape[1:], F32)
+        DVT[h] = jnp.zeros(DVT.shape[1:], F32)
+
+    lane = lax.broadcasted_iota(jnp.int32, (TILE, 128), 1)
+    low_lane = jnp.where(lane >= 64, lane - 64, lane)
+
+    def tables(base, group):
+        cosine, sine = COS[pl.ds(base, TILE), :], SIN[pl.ds(base, TILE), :]
+        if group == 1:
+            cosine = jnp.where(lane >= 64, cosine, 1.0)
+            sine = jnp.where(lane >= 64, sine, 0.0)
+        if group == 2:
+            cosine = jnp.where(lane < 64, cosine, 1.0)
+            sine = jnp.where(lane < 64, sine, 0.0)
+        upper = jnp.where(low_lane >= ROT // 2, sine, 0.0)
+        return cosine, upper, sine - upper
+
+    def norm_rows(base, count):
+        raw = T[pl.ds(base, count), :].astype(F32)
+        centred = raw - jnp.mean(raw, axis=1, keepdims=True)
+        inverse_root = lax.rsqrt(jnp.mean(centred * centred, axis=1, keepdims=True) + epsilon)
+        return centred * inverse_root, inverse_root
+
+    def forward_block(block):
+        base = pl.multiple_of(block * rows, rows)
+
+        @pl.loop(0, rows // 64)
+        def _(part):
+            off = pl.multiple_of(base + part * 64, 64)
+            normed, _ = norm_rows(off, 64)
+            AI[pl.ds(off, 64), :] = (normed * ga[...] + ba[...]).astype(BF16)
+            FI[pl.ds(off, 64), :] = (normed * gm[...] + bm[...]).astype(BF16)
+
+        for group in range(3 * heads // 2):
+            if group % 2 == 0:
+                columns = slice(group * 128, group * 128 + 256)
+                pair = dot_nn(AI[pl.ds(base, rows), :], WQKV[:, columns]) + bqkv[:, columns]
+            value = pair[:, (group % 2) * 128 : (group % 2) * 128 + 128]
+            cosine, upper, lower = tables(base, group % 3)
+            turned = (
+                value * cosine
+                - lower * pltpu.roll(value, 128 - ROT // 2, 1)
+                + upper * pltpu.roll(value, ROT // 2, 1)
+            ).astype(BF16)
+            first = 2 * (group // 3)
+            left, left_head = ((QH, first), (VH, first), (KH, first + 1))[group % 3]
+            right, right_head = ((KH, first), (QH, first + 1), (VH, first + 1))[group % 3]
+            left[left_head, pl.ds(base, rows), :] = turned[:, :HD]
+            right[right_head, pl.ds(base, rows), :] = turned[:, HD:]
+
+        @pl.loop(0, hidden_width // TILE)
+        def _(part):
+            columns = pl.ds(pl.multiple_of(part * TILE, TILE), TILE)
+            preact = dot_nn(FI[pl.ds(base, rows), :], WUP[:, columns]) + bup[:, columns]
+            cdf = 0.5 * (1.0 + lax.erf(preact * 0.5**0.5))
+            density = jnp.exp(-0.5 * preact * preact) * (1.0 / math.sqrt(2.0 * math.pi))
+            HID[pl.ds(base, rows), columns] = (preact * cdf).astype(BF16)
+            GP[pl.ds(base, rows), columns] = cdf + preact * density
+
+    def cotangent_block(block):
+        base = pl.multiple_of(block * rows, rows)
+        upstream = C[pl.ds(base, rows), :]
+        grad = dot_nt(upstream, WOUT[...]).astype(BF16)
+        for h in range(heads):
+            CGH[h, pl.ds(base, rows), :] = grad[:, h * HD : (h + 1) * HD]
+
+        @pl.loop(0, hidden_width // TILE)
+        def _(part):
+            columns = pl.ds(pl.multiple_of(part * TILE, TILE), TILE)
+            back = dot_nt(C[pl.ds(base, rows), :], WDN[columns, :])
+            rounded = (back * GP[pl.ds(base, rows), columns]).astype(BF16)
+            PG[pl.ds(base, rows), columns] = rounded
+            SV[6:7, columns] += jnp.sum(rounded.astype(F32), axis=0, keepdims=True)
+
+    def attention_unit(unit):
+        h = lax.div(unit, blocks)
+        own = lax.rem(unit, blocks)
+        here = pl.ds(pl.multiple_of(own * TILE, TILE), TILE)
+        query = QH[h, here, :]
+        grad = CGH[h, here, :]
+        query_t = query.astype(F32).T.astype(BF16)
+        grad_t = grad.astype(F32).T.astype(BF16)
+
+        def place(number):
+            return pl.ds(pl.multiple_of(number * TILE, TILE), TILE)
+
+        def raw(number):
+            return dot_nt(query, KH[h, place(number), :]) * scale
+
+        def first(number, top):
+            scores = raw(number)
+            SCO[:, place(number)] = scores
+            return jnp.maximum(top, jnp.max(scores, axis=1, keepdims=True))
+
+        top = lax.fori_loop(0, own, first, jnp.full((TILE, 1), -1e30, F32))
+        row_at = lax.broadcasted_iota(jnp.int32, (TILE, TILE), 0)
+        column_at = lax.broadcasted_iota(jnp.int32, (TILE, TILE), 1)
+        scores = jnp.where(column_at <= row_at, raw(own), -1e30)
+        SCO[:, here] = scores
+        top = jnp.maximum(top, jnp.max(scores, axis=1, keepdims=True))
+
+        def second(number, total):
+            weights = jnp.exp(SCO[:, place(number)] - top)
+            SCO[:, place(number)] = weights
+            return total + jnp.sum(weights, axis=1, keepdims=True)
+
+        total = lax.fori_loop(0, own + 1, second, jnp.zeros((TILE, 1), F32))
+        inverse = 1.0 / total
+
+        def third(number, carried):
+            context, delta = carried
+            probs = SCO[:, place(number)] * inverse
+            value = VH[h, place(number), :]
+            context = context + dot_nn(probs.astype(BF16), value)
+            prob_grad = dot_nt(grad, value)
+            SCO[:, place(number)] = probs
+            DPS[:, place(number)] = prob_grad
+            return context, delta + jnp.sum(probs * prob_grad, axis=1, keepdims=True)
+
+        context, delta = lax.fori_loop(
+            0, own + 1, third, (jnp.zeros((TILE, HD), F32), jnp.zeros((TILE, 1), F32))
+        )
+        CTXH[h, here, :] = context.astype(BF16)
+
+        def fourth(number, query_grad):
+            probs = SCO[:, place(number)]
+            score_grad = (probs * (DPS[:, place(number)] - delta)).astype(BF16)
+            DKT[h, :, place(number)] += dot_nn(query_t, score_grad)
+            DVT[h, :, place(number)] += dot_nn(grad_t, probs.astype(BF16))
+            return query_grad + dot_nn(score_grad, KH[h, place(number), :])
+
+        DQ[h, here, :] = scale * lax.fori_loop(0, own + 1, fourth, jnp.zeros((TILE, HD), F32))
+
+    def assemble(block):
+        base = pl.multiple_of(block * TILE, TILE)
+        here = pl.ds(base, TILE)
+        for pair in range(heads // 2):
+            one, two = 2 * pair, 2 * pair + 1
+            CTX[here, pair * 128 : (pair + 1) * 128] = jnp.concatenate(
+                [CTXH[one, here, :], CTXH[two, here, :]], axis=1
+            )
+            parts = [
+                (DQ[one, here, :], scale * DKT[one, :, here].T),
+                (DVT[one, :, here].T, DQ[two, here, :]),
+                (scale * DKT[two, :, here].T, DVT[two, :, here].T),
+            ]
+            for group, (left, right) in enumerate(parts):
+                grad = jnp.concatenate([left, right], axis=1)
+                cosine, upper, lower = tables(base, group)
+                turned = (
+                    grad * cosine
+                    + pltpu.roll(grad * upper, 128 - ROT // 2, 1)
+                    - pltpu.roll(grad * lower, ROT // 2, 1)
+                ).astype(BF16)
+                columns = slice((3 * pair + group) * 128, (3 * pair + group + 1) * 128)
+                QG[here, columns] = turned
+                SV[7:8, columns] += jnp.sum(turned.astype(F32), axis=0, keepdims=True)
+
+    def order(step):
+        flip_core = 1 - lax.div(step, 2)
+        flip_x = 1 - lax.rem(step, 2)
+        return 2 * lax.rem(x + flip_x, 2) + lax.rem(core + flip_core, 2)
+
+    def to_core(which, slot):
+        block = (2 * x + 1 - core) if slot == 0 else (2 * (1 - x) + 1 - core)
+        return remote(
+            PART.at[which, pl.ds(block * rows, rows)], RA.at[which, slot],
+            b_s.at[which, slot], b_r.at[which, slot], core_mate,
+        )
+
+    def to_x(which):
+        return remote(
+            PART.at[which, pl.ds(x_block * rows, rows)], RB.at[which],
+            b_s.at[which, 2], b_r.at[which, 2], x_mate,
+        )
+
+    def send_after(which, step):
+        @pl.when(step == 0)
+        def _():
+            to_core(which, 1).start()
+
+        @pl.when(step == 1)
+        def _():
+            to_core(which, 0).start()
+
+    def branch_block(step):
+        base = pl.multiple_of(order(step) * rows, rows)
+        here = pl.ds(base, rows)
+
+        @pl.loop(0, width // TILE)
+        def _(part):
+            columns = pl.ds(pl.multiple_of(part * TILE, TILE), TILE)
+            PART[0, here, columns] = (
+                dot_nn(CTX[here, :], WOUT[:, columns]) + dot_nn(HID[here, :], WDN[:, columns])
+            ).astype(BF16)
+
+        send_after(0, step)
+
+    def back_block(step):
+        base = pl.multiple_of(order(step) * rows, rows)
+        here = pl.ds(base, rows)
+        raw = T[here, :].astype(F32)
+        average = jnp.mean(raw, axis=1, keepdims=True)
+        spread = jnp.mean((raw - average) * (raw - average), axis=1, keepdims=True)
+        inverse_root = lax.rsqrt(spread + epsilon)
+
+        @pl.loop(0, width // TILE)
+        def _(part):
+            columns = pl.ds(pl.multiple_of(part * TILE, TILE), TILE)
+            normed = (T[here, columns].astype(F32) - average) * inverse_root
+            attention_back = dot_nt(QG[here, :], WQKV[columns, :])
+            feed_back = dot_nt(PG[here, :], WUP[columns, :])
+            SV[0:1, columns] += jnp.sum(normed * attention_back, axis=0, keepdims=True)
+            SV[1:2, columns] += jnp.sum(attention_back, axis=0, keepdims=True)
+            SV[2:3, columns] += jnp.sum(normed * feed_back, axis=0, keepdims=True)
+            SV[3:4, columns] += jnp.sum(feed_back, axis=0, keepdims=True)
+            PART[1, here, columns] = (attention_back * ga[:, columns] + feed_back * gm[:, columns]).astype(BF16)
+
+        send_after(1, step)
+
+    def chip_sum(which):
+        to_core(which, 1).wait_recv()
+        there = pl.ds(pl.multiple_of(x_block * rows, rows), rows)
+        PART[which, there, :] = (PART[which, there, :].astype(F32) + RA[which, 1].astype(F32)).astype(BF16)
+        to_x(which).start()
+
+    def finish():
+        for which in range(2):
+            to_core(which, 0).wait_recv()
+            to_x(which).wait_recv()
+        SV[4:5, :] = jnp.sum(C[pl.ds(t * rows, rows), :].astype(F32), axis=0, keepdims=True)
+
+        def total(which, off):
+            return (
+                PART[which, pl.ds(pl.multiple_of(t * rows + off, 64), 64), :].astype(F32)
+                + RA[which, 0, pl.ds(off, 64), :].astype(F32)
+                + RB[which, pl.ds(off, 64), :].astype(F32)
+            )
+
+        def square(value):
+            return jnp.sum(jnp.sum(value * value, axis=1, keepdims=True), axis=0, keepdims=True)
+
+        def part(number, sums):
+            off = pl.multiple_of(number * 64, 64)
+            here = pl.ds(pl.multiple_of(t * rows + off, 64), 64)
+            branch = total(0, off) + bo[...] + bd[...]
+            residual = T[here, :].astype(F32) + branch
+            mixed[pl.ds(off, 64), :] = residual.astype(BF16)
+            normed, inverse_root = norm_rows(t * rows + off, 64)
+            grad = total(1, off)
+            grad = inverse_root * (
+                grad
+                - jnp.mean(grad, axis=1, keepdims=True)
+                - normed * jnp.mean(grad * normed, axis=1, keepdims=True)
+            ) + C[here, :].astype(F32)
+            igrad[pl.ds(off, 64), :] = grad
+            return sums[0] + square(residual), sums[1] + square(branch), sums[2] + square(grad)
+
+        zero = jnp.zeros((1, 1), F32)
+        sums = lax.fori_loop(0, rows // 64, part, (zero, zero, zero))
+        spot = lax.broadcasted_iota(jnp.int32, (1, width), 1)
+        SV[5:6, :] = jnp.where(
+            spot == 0, sums[0], jnp.where(spot == 1, sums[1], jnp.where(spot == 2, sums[2], 0.0))
+        )
+
+    def exchange(step):
+        mate = (
+            core_mate,
+            x_mate,
+            (dp + 1 - 2 * y, t),
+            (2 * (z + 1 - 2 * lax.rem(z, 2)) + y, t),
+            (2 * lax.rem(z + 2, depth) + y, t),
+        )[step]
+        return remote(ES.at[step], EX.at[step], e_s.at[step], e_r.at[step], mate)
+
+    def exchange_send(step):
+        ES[step] = SV[...]
+        exchange(step).start()
+
+    def exchange_receive(step):
+        exchange(step).wait_recv()
+        if step < 2:
+            row = lax.broadcasted_iota(jnp.int32, SV.shape, 0)
+            SV[...] += jnp.where(row < 6, EX[step], 0.0)
+        else:
+            SV[...] += EX[step]
+
+    def chunk(direction, step):
+        return lax.rem(at + ring - step, ring) if direction == 0 else lax.rem(at + step, ring)
+
+    def gathered(direction, step):
+        return lax.rem(at + 1 + ring - step, ring) if direction == 0 else lax.rem(at + ring - 1 + step, ring)
+
+    def own_partial(segment, step):
+        for direction in range(2):
+            number = chunk(direction, step)
+            columns = pl.ds(pl.multiple_of(number * 128, 128), 128)
+            if segment < 2:
+                left, right = (HID, C) if segment == 0 else (FI, PG)
+                PSC[direction] = dot_tn(left[:, columns], right[:, direction * 512 : (direction + 1) * 512])
+            else:
+                PSC[direction, :, 0:384] = dot_tn(AI[:, columns], QG[:, direction * 384 : (direction + 1) * 384])
+                PSC[direction, :, 384:512] = dot_tn(
+                    CTX[:, direction * 128 : (direction + 1) * 128], C[:, columns]
+                )
+
+    def scatter(segment, direction, half, step):
+        return remote(
+            RSB.at[segment, direction, half, step], RSB.at[segment, direction, half, step + 1],
+            r_s.at[segment, direction, half, step], r_r.at[segment, direction, half, step], onward[direction],
+        )
+
+    def collect(segment, direction, half, step):
+        piece = GB.at[segment, direction, half, gathered(direction, step)]
+        sem = ring - 1 + step
+        return remote(
+            piece, piece,
+            r_s.at[segment, direction, half, sem], r_r.at[segment, direction, half, sem], onward[direction],
+        )
+
+    pieces = [(half, direction) for half in range(2) for direction in range(2)]
+
+    def ring_open(segment):
+        own_partial(segment, 0)
+        for half, direction in pieces:
+            RSB[segment, direction, half, 0] = PSC[direction, :, half * 256 : (half + 1) * 256].astype(BF16)
+            scatter(segment, direction, half, 0).start()
+
+    def ring_scatter(segment, step):
+        for half, direction in pieces:
+            scatter(segment, direction, half, step - 1).wait_recv()
+            RSB[segment, direction, half, step] = (
+                RSB[segment, direction, half, step].astype(F32)
+                + PSC[direction, :, half * 256 : (half + 1) * 256]
+            ).astype(BF16)
+            scatter(segment, direction, half, step).start()
+
+    def ring_turn(segment):
+        last = ring - 1
+        for half, direction in pieces:
+            scatter(segment, direction, half, last - 1).wait_recv()
+            GB[segment, direction, half, gathered(direction, 0)] = (
+                RSB[segment, direction, half, last].astype(F32)
+                + PSC[direction, :, half * 256 : (half + 1) * 256]
+            ).astype(BF16)
+            collect(segment, direction, half, 0).start()
+
+    def ring_collect(segment, step):
+        for half, direction in pieces:
+            collect(segment, direction, half, step - 1).wait_recv()
+            collect(segment, direction, half, step).start()
+
+    def ring_close(segment):
+        for half, direction in pieces:
+            collect(segment, direction, half, ring - 2).wait_recv()
+
+    def out_copies(segment, direction, half, number):
+        piece = GB.at[segment, direction, half, number]
+        there = pl.ds(number * 128, 128)
+        sem = o_s.at[segment, direction, half, number]
+        if segment < 2:
+            out = gd_o if segment == 0 else gu_o
+            return [pltpu.make_async_copy(piece, out.at[there, pl.ds(direction * 512 + half * 256, 256)], sem)]
+        if half == 0:
+            return [pltpu.make_async_copy(piece, gq_o.at[there, pl.ds(direction * 384, 256)], sem)]
+        return [
+            pltpu.make_async_copy(
+                piece.at[:, pl.ds(0, 128)], gq_o.at[there, pl.ds(direction * 384 + 256, 128)], sem
+            ),
+            pltpu.make_async_copy(
+                piece.at[:, pl.ds(128, 128)], go_o.at[pl.ds(direction * 128, 128), there], p_s.at[direction, number]
+            ),
+        ]
+
+    def ring_out(segment, action):
+        @pl.loop(0, ring)
+        def _(number):
+            for half, direction in pieces:
+                for copy in out_copies(segment, direction, half, number):
+                    getattr(copy, action)()
+
+    local[0].wait()
+    local[2].wait()
+    local[3].wait()
+
+    @pl.loop(0, 4)
+    def _(step):
+        @pl.when(step == 1)
+        def _():
+            gather(0, 0).wait_recv()
+
+        @pl.when(step == 2)
+        def _():
+            gather(0, 1).wait_recv()
+            gather(0, 3).start()
+            gather(0, 2).wait_recv()
+            gather(0, 4).start()
+            gather(1, 1).start()
+            gather(1, 2).start()
+            gather(1, 0).start()
+
+        @pl.when(step == 3)
+        def _():
+            gather(0, 3).wait_recv()
+            gather(0, 4).wait_recv()
+
+        forward_block(2 * lax.rem(x + lax.div(step, 2), 2) + lax.rem(core + lax.rem(step, 2), 2))
+
+    local[1].wait()
+    local[4].wait()
+    local[5].wait()
+    gather(1, 1).wait_recv()
+    gather(1, 3).start()
+    gather(1, 0).wait_recv()
+    gather(1, 2).wait_recv()
+    gather(1, 4).start()
+    gather(1, 3).wait_recv()
+    gather(1, 4).wait_recv()
+
+    turns = ring - 1
+
+    def during(condition, work):
+        pl.when(condition)(work)
+
+    ring_open(0)
+
+    @pl.loop(1, turns)
+    def _(step):
+        own_partial(0, step)
+        during(step <= 4, lambda: cotangent_block(step - 1))
+        during(step > 4, lambda: attention_unit(step - 5))
+        ring_scatter(0, step)
+
+    own_partial(0, turns)
+    ring_turn(0)
+
+    @pl.loop(1, turns)
+    def _(step):
+        attention_unit(step + 1)
+        ring_collect(0, step)
+
+    ring_open(1)
+    ring_close(0)
+    ring_out(0, "start")
+
+    @pl.loop(1, turns)
+    def _(step):
+        own_partial(1, step)
+        attention_unit(step + 7)
+        ring_scatter(1, step)
+
+    own_partial(1, turns)
+    ring_turn(1)
+
+    @pl.loop(1, turns)
+    def _(step):
+        during(step <= 2, lambda: attention_unit(step + 13))
+        during(step > 2, lambda: assemble(step - 3))
+        ring_collect(1, step)
+
+    ring_open(2)
+    ring_close(1)
+    ring_out(1, "start")
+
+    @pl.loop(1, turns)
+    def _(step):
+        own_partial(2, step)
+        during(step <= 4, lambda: branch_block(step - 1))
+        during(step > 4, lambda: back_block(step - 5))
+        during(step == 6, lambda: chip_sum(0))
+        ring_scatter(2, step)
+
+    own_partial(2, turns)
+    ring_turn(2)
+
+    @pl.loop(1, turns)
+    def _(step):
+        during(step <= 2, lambda: back_block(step + 1))
+        during(step == 3, lambda: chip_sum(1))
+        during(step == 6, finish)
+        ring_collect(2, step)
+
+    exchange_send(0)
+    ring_close(2)
+    ring_out(2, "start")
+    exchange_receive(0)
+    for step in range(1, 5):
+        exchange_send(step)
+        exchange_receive(step)
+    sv_o[...] = SV[...]
+
+    for which in range(2):
+        for kind in range(5):
+            gather(which, kind).wait_send()
+        for slot in range(2):
+            to_core(which, slot).wait_send()
+        to_x(which).wait_send()
+    for step in range(5):
+        exchange(step).wait_send()
+    for segment in range(3):
+
+        @pl.loop(0, ring - 1)
+        def _(step):
+            for half, direction in pieces:
+                scatter(segment, direction, half, step).wait_send()
+                collect(segment, direction, half, step).wait_send()
+
+        ring_out(segment, "wait")
+
+
+def angle_parts(seq_len):
+    inverse = 10000.0 ** (-(np.arange(ROT // 2) * 2.0 / ROT))
+    per_lane = np.zeros((128,))
+    for start in (0, ROT // 2, HD, HD + ROT // 2):
+        per_lane[start : start + ROT // 2] = inverse
+    coarse = (np.arange(seq_len // 32) * 32.0)[:, None] * per_lane[None, :]
+    fine = np.arange(32.0)[:, None] * per_lane[None, :]
+    return [f(a).astype(np.float32) for a in (coarse, fine) for f in (np.cos, np.sin)]
+
+
+def per_device_fused(
+    tokens, cotangent, gain_attn, bias_attn, gain_mlp, bias_mlp, qkv_weight, qkv_bias,
+    out_weight, out_bias, up_weight, up_bias, down_weight, down_bias,
+):
+    rows, width = tokens.shape
+    ring = lax.axis_size("dp")
+    seq = rows * lax.axis_size("tensor")
+    heads = out_weight.shape[0] // HD
+    hidden_width = up_weight.shape[1]
+    qkv_width = qkv_weight.shape[1]
+    cos_a, sin_a, cos_b, sin_b = angle_parts(seq)
+    vmem = pl.BlockSpec(memory_space=pltpu.VMEM)
+    hbm = pl.BlockSpec(memory_space=pl.ANY)
+    V = pltpu.VMEM
+    D = pltpu.SemaphoreType.DMA
+    scratch = [
+        V((seq, width), BF16), V((seq, width), BF16), V((seq, width), BF16), V((seq, width), BF16),
+        V((seq, hidden_width), BF16), V((seq, hidden_width), F32), V((seq, hidden_width), BF16),
+        V((seq, qkv_width), BF16),
+        V((heads, seq, HD), BF16), V((heads, seq, HD), BF16), V((heads, seq, HD), BF16),
+        V((heads, seq, HD), BF16), V((heads, seq, HD), BF16), V((seq, heads * HD), BF16),
+        V((heads, seq, HD), F32), V((heads, HD, seq), F32), V((heads, HD, seq), F32),
+        V((TILE, seq), F32), V((TILE, seq), F32),
+        V((seq, 128), F32), V((seq, 128), F32),
+        V(qkv_weight.shape, BF16), V(out_weight.shape, BF16), V(up_weight.shape, BF16), V(down_weight.shape, BF16),
+        V((3, 2, 2, ring, 128, 256), BF16), V((3, 2, 2, ring, 128, 256), BF16), V((2, 128, 512), F32),
+        V((2, seq, width), BF16), V((2, 2, rows, width), BF16), V((2, rows, width), BF16),
+        V((8, width), F32), V((5, 8, width), F32), V((5, 8, width), F32),
+        D((6,)), D((2, 5)), D((2, 5)),
+        D((3, 2, 2, 2 * ring - 2)), D((3, 2, 2, 2 * ring - 2)),
+        D((2, 3)), D((2, 3)), D((5,)), D((5,)), D((3, 2, 2, ring)), D((2, ring)),
+    ]
+    mixed, input_grad, gd, gu, gq, go, sv = pl.pallas_call(
+        functools.partial(fused_kernel, ring),
+        out_shape=[
+            jax.ShapeDtypeStruct((rows, width), BF16),
+            jax.ShapeDtypeStruct((rows, width), F32),
+            jax.ShapeDtypeStruct(down_weight.shape, BF16),
+            jax.ShapeDtypeStruct(up_weight.shape, BF16),
+            jax.ShapeDtypeStruct(qkv_weight.shape, BF16),
+            jax.ShapeDtypeStruct(out_weight.shape, BF16),
+            jax.ShapeDtypeStruct((8, width), F32),
+        ],
+        in_specs=[hbm, hbm] + [vmem] * 8 + [hbm] * 4 + [vmem] * 4,
+        out_specs=[vmem, vmem, hbm, hbm, hbm, hbm, vmem],
+        scratch_shapes=scratch,
+        compiler_params=pltpu.CompilerParams(has_side_effects=True, vmem_limit_bytes=VMEM_LIMIT),
+        name="layer",
+    )(
+        tokens, cotangent,
+        *(v.reshape(1, -1) for v in (gain_attn, bias_attn, gain_mlp, bias_mlp, out_bias, down_bias, qkv_bias, up_bias)),
+        qkv_weight, out_weight, up_weight, down_weight, cos_a, sin_a, cos_b, sin_b,
+    )
+    elements = rows * width * ring * lax.axis_size("tensor")
+    statistics = jnp.sqrt(sv[5, :3] / elements)
+    return (
+        mixed, input_grad, sv[0], sv[1], sv[2], sv[3],
+        gq.astype(F32), sv[7, :qkv_width], go.astype(F32), sv[4],
+        gu.astype(F32), sv[6], gd.astype(F32), sv[4], statistics,
+    )
+
+
 def solution(mesh):
     in_specs = (
         P(("dp", "tensor"), None),
@@ -293,6 +978,7 @@
         P(),
         P(),
     )
+    fused = mesh.shape["tensor"] == 4 and mesh.shape["dp"] == 8
     return jax.shard_map(
-        per_device, mesh=mesh, in_specs=in_specs, out_specs=out_specs, check_vma=False
-    )
+        per_device_fused if fused else per_device, mesh=mesh, in_specs=in_specs, out_specs=out_specs, check_vma=False
+    )

time: 687 us -> 235 us (0.34); the launches traced: 678 us -> 234 us
  waiting for transfers between devices: 410 us -> 0 us
  Pallas kernels: 0 us -> 216 us
  matrix products: 103 us -> 0 us
  blocking collectives: 64.7 us -> 0 us
  local copies, waits for them, and re-layouts: 53.5 us -> 6.59 us
  other arithmetic: 28.8 us -> 10.9 us
  between operations: 14.8 us -> 0.66 us
    psum x1 -> x0, waiting for transfers between devices: 355 us -> none  [per_device(): lax.psum((qkv_weight_grad, qkv_bias_grad, out_weight_grad, up_weight_grad...]
    pallas_call x0 -> x1, Pallas kernels: none -> 216 us  [per_device_fused(): pl.pallas_call(functools.partial(fused_kernel, ring), out_shape=[jax.Shap...]
    dot_general x26 -> x0, matrix products: 103 us -> none  [the longest x4 13.9 us: against(): lax.dot_general(left, right, (((1,), (1,)), ((), ())), preferred_element_...]
    psum x2 -> x0, blocking collectives: 64.7 us -> none  [the longest x1 42.6 us: per_device(): lax.psum((gain_terms, bias_rows, grad_square), ('dp', 'tensor'))]
    reduce_scatter x2 -> x0, waiting for transfers between devices: 27.4 us -> none  [the longest x1 27.4 us: per_device(): lax.psum_scatter(jnp.dot(context_rows, out_weight, preferred_element_type...]
    all_gather x2 -> x0, waiting for transfers between devices: 25.9 us -> none  [the longest x1 25.9 us: per_device(): whole_rows = lax.all_gather(tokens, 'tensor', axis=0, tiled=True)]
    dynamic_update_slice x4 -> x0, local copies, waits for them, and re-layouts: 23.5 us -> none  [per_device(): lax.scan(backward_block, (empty, empty), jnp.arange(block_total, dtype=jn...]
    reduce_sum x9 -> x0, other arithmetic: 16.3 us -> none  [the longest x2 4.67 us: forward_block(): totals = jnp.sum(weights, axis=-1, keepdims=True)]
  transfers between devices with their start and end apart: 5 -> 0, of which waited for: 3 -> 0; matrix products, arithmetic and copies ran while one was open for 10% -> 0% of each run, Pallas kernels for 0% -> 0%
where the time goes in v1:
time: 235 us; the launch traced here: 234 us
  Pallas kernels  216 us (92%)
  other arithmetic  10.9 us (5%)
  local copies, waits for them, and re-layouts  6.59 us (3%)
    pallas_call x1, Pallas kernels, per_device_fused(): pl.pallas_call(functools.partial(fused_kernel, ring), out_shape=[jax.Shap...  216 us

profile of v1, /device:TPU:0, one launch (start us, length us, event | category | flops | bytes accessed | tf_op | source)
XLA Modules:
  0.0 234.4 jit_solution(14819255666431128296)
XLA Ops:
  0.6 1.3 reshape.63.bqkv
  1.9 216.3 %layer.1 = (bf16[256,1024]{1,0:T(8,128)(2,1)}, f32[256,1024]{1,0:T(8,128)}, bf16[1024,1024]{1,0:T(8,128)(2,1)}, bf16[1024,1024]{1,0:T(8,128)(2,1)}, bf16[1024,76...) custom-call(bf16[256,1024]{1,0:T(8,128)(2,1)} %tok.1, bf16[256,1024]{1,0:T(8,128)(2,1)} %cot.1, ...), custom_call_target="tpu_custom_call" | custom-call | tf_op jit(solution)/shard_map/layer/pallas_call | solution.py:917
  218.2 1.6 fusion
  219.8 0.0 copy-start.5
  219.8 1.3 slice_reduce_fusion
  221.2 1.2 sqrt_bitcast_fusion
  222.4 0.0 copy-start
  222.4 4.2 %convert_element_type.14 = f32[1024,1024]{1,0:T(8,128)} convert(bf16[1024,1024]{1,0:T(8,128)(2,1)} %get-tuple-element.27) | non-fusion elementwise | flops 1048576 | bytes 6291456 | tf_op jit(solution)/shard_map/convert_element_type | solution.py:943
  226.6 0.0 copy-done
  226.6 0.0 copy-start.1
  226.6 2.5 %convert_element_type.15 = f32[1024,1024]{1,0:T(8,128)} convert(bf16[1024,1024]{1,0:T(8,128)(2,1)S(1)} %copy-done) | non-fusion elementwise | flops 1048576 | bytes 6291456 | tf_op jit(solution)/shard_map/convert_element_type | solution.py:943
  229.1 0.0 copy-done.1
  229.1 0.0 copy-start.3
  229.1 0.0 copy-start.4
  229.1 1.9 convert_element_type.12
  231.0 0.0 copy-start.2
  231.0 0.0 copy-done.3
  231.0 1.1 convert_element_type.13
  232.1 0.0 copy-done.5
  232.1 0.6 copy.36
  232.7 0.0 copy-done.4
  232.7 0.8 copy.37
  233.5 0.0 copy-done.2
  233.5 1.0 copy.38
Async XLA Ops:
  219.8 12.2 %copy-start.5 = (f32[1,1024]{1,0:T(1,128)}, f32[1,1024]{1,0:T(1,128)S(1)}, u32[]{:S(2)}) copy-start(f32[1,1024]{1,0:T(1,128)S(1)} %get-tuple-element.30) | copy-start | bytes 12292
  222.4 4.2 %copy-start = (bf16[1024,1024]{1,0:T(8,128)(2,1)S(1)}, bf16[1024,1024]{1,0:T(8,128)(2,1)}, u32[]{:S(2)}) copy-start(bf16[1024,1024]{1,0:T(8,128)(2,1)} %get-tuple-element.28) | copy-start | bytes 6291460
  226.6 2.5 %copy-start.1 = (bf16[1024,768]{1,0:T(8,128)(2,1)S(1)}, bf16[1024,768]{1,0:T(8,128)(2,1)}, u32[]{:S(2)}) copy-start(bf16[1024,768]{1,0:T(8,128)(2,1)} %get-tuple-element.25) | copy-start | bytes 4718596
  229.1 1.9 copy-start.3
  229.1 3.6 %copy-start.4 = (bf16[256,1024]{1,0:T(8,128)(2,1)S(1)}, bf16[256,1024]{1,0:T(8,128)(2,1)}, u32[]{:S(2)}) copy-start(bf16[256,1024]{1,0:T(8,128)(2,1)} %get-tuple-element.80) | copy-start | bytes 1572868
  231.0 2.5 %copy-start.2 = (f32[256,1024]{1,0:T(8,128)S(1)}, f32[256,1024]{1,0:T(8,128)}, u32[]{:S(2)}) copy-start(f32[256,1024]{1,0:T(8,128)} %get-tuple-element.81) | copy-start | bytes 3145732

commit v2 on v1

--- a/solution.py
+++ b/solution.py
@@ -268,7 +268,7 @@
 BF16 = jnp.bfloat16
 MESH = pl.DeviceIdType.MESH
 TILE = 256
-RING_X = 4
+PARTS = 4
 
 
 def dot_nn(left, right):
@@ -287,9 +287,9 @@
     ring,
     tok, cot, ga, ba, gm, bm, bo, bd, bqkv, bup, wqkv_h, wout_h, wup_h, wdn_h, cos_a, sin_a, cos_b, sin_b,
     mixed, igrad, gd_o, gu_o, gq_o, go_o, sv_o,
-    T, C, AI, FI, HID, GP, PG, QG, QH, KH, VH, CGH, CTXH, CTX, DQ, DKT, DVT, SCO, DPS, COS, SIN,
+    T, C, AI, FI, HID, GP, PG, QG, QH, KH, VH, CGH, CTXH, CTX, DQ, DKT, DVT, COS, SIN,
     WQKV, WOUT, WUP, WDN, RSB, GB, PSC, PART, RA, RB, SV, ES, EX,
-    lsem, g_s, g_r, r_s, r_r, b_s, b_r, e_s, e_r, o_s, p_s,
+    lsem, g_s, g_r, r_s, r_r, b_s, b_r, e_s, e_r, o_s,
 ):
     rows = tok.shape[0]
     width = tok.shape[1]
@@ -348,6 +348,9 @@
     gather(0, 1).start()
     gather(0, 2).start()
     gather(0, 0).start()
+    gather(1, 1).start()
+    gather(1, 2).start()
+    gather(1, 0).start()
     for copy in (local[0], local[2], local[3], local[1], local[4], local[5]):
         copy.start()
 
@@ -412,9 +415,8 @@
             left[left_head, pl.ds(base, rows), :] = turned[:, :HD]
             right[right_head, pl.ds(base, rows), :] = turned[:, HD:]
 
-        @pl.loop(0, hidden_width // TILE)
-        def _(part):
-            columns = pl.ds(pl.multiple_of(part * TILE, TILE), TILE)
+        for part in range(hidden_width // TILE):
+            columns = slice(part * TILE, (part + 1) * TILE)
             preact = dot_nn(FI[pl.ds(base, rows), :], WUP[:, columns]) + bup[:, columns]
             cdf = 0.5 * (1.0 + lax.erf(preact * 0.5**0.5))
             density = jnp.exp(-0.5 * preact * preact) * (1.0 / math.sqrt(2.0 * math.pi))
@@ -428,72 +430,41 @@
         for h in range(heads):
             CGH[h, pl.ds(base, rows), :] = grad[:, h * HD : (h + 1) * HD]
 
-        @pl.loop(0, hidden_width // TILE)
-        def _(part):
-            columns = pl.ds(pl.multiple_of(part * TILE, TILE), TILE)
-            back = dot_nt(C[pl.ds(base, rows), :], WDN[columns, :])
+        for part in range(hidden_width // TILE):
+            columns = slice(part * TILE, (part + 1) * TILE)
+            back = dot_nt(upstream, WDN[columns, :])
             rounded = (back * GP[pl.ds(base, rows), columns]).astype(BF16)
             PG[pl.ds(base, rows), columns] = rounded
             SV[6:7, columns] += jnp.sum(rounded.astype(F32), axis=0, keepdims=True)
 
+    def attention_rows(h, own):
+        here = slice(own * TILE, (own + 1) * TILE)
+        before = own * TILE
+        reach = before + TILE
+        query = QH[h, here, :]
+        grad = CGH[h, here, :]
+        keys = KH[h, :reach, :]
+        values = VH[h, :reach, :]
+        scores = dot_nt(query, keys) * scale
+        row_at = lax.broadcasted_iota(jnp.int32, (TILE, TILE), 0)
+        column_at = lax.broadcasted_iota(jnp.int32, (TILE, TILE), 1)
+        corner = jnp.where(column_at <= row_at, scores[:, before:], -1e30)
+        scores = jnp.concatenate([scores[:, :before], corner], axis=1) if own else corner
+        weights = jnp.exp(scores - jnp.max(scores, axis=1, keepdims=True))
+        probs = weights * (1.0 / jnp.sum(weights, axis=1, keepdims=True))
+        soft = probs.astype(BF16)
+        CTXH[h, here, :] = dot_nn(soft, values).astype(BF16)
+        prob_grad = dot_nt(grad, values)
+        delta = jnp.sum(probs * prob_grad, axis=1, keepdims=True)
+        score_grad = (probs * (prob_grad - delta)).astype(BF16)
+        DQ[h, here, :] = scale * dot_nn(score_grad, keys)
+        DKT[h, :, :reach] += dot_nn(query.astype(F32).T.astype(BF16), score_grad)
+        DVT[h, :, :reach] += dot_nn(grad.astype(F32).T.astype(BF16), soft)
+
     def attention_unit(unit):
         h = lax.div(unit, blocks)
-        own = lax.rem(unit, blocks)
-        here = pl.ds(pl.multiple_of(own * TILE, TILE), TILE)
-        query = QH[h, here, :]
-        grad = CGH[h, here, :]
-        query_t = query.astype(F32).T.astype(BF16)
-        grad_t = grad.astype(F32).T.astype(BF16)
-
-        def place(number):
-            return pl.ds(pl.multiple_of(number * TILE, TILE), TILE)
-
-        def raw(number):
-            return dot_nt(query, KH[h, place(number), :]) * scale
-
-        def first(number, top):
-            scores = raw(number)
-            SCO[:, place(number)] = scores
-            return jnp.maximum(top, jnp.max(scores, axis=1, keepdims=True))
-
-        top = lax.fori_loop(0, own, first, jnp.full((TILE, 1), -1e30, F32))
-        row_at = lax.broadcasted_iota(jnp.int32, (TILE, TILE), 0)
-        column_at = lax.broadcasted_iota(jnp.int32, (TILE, TILE), 1)
-        scores = jnp.where(column_at <= row_at, raw(own), -1e30)
-        SCO[:, here] = scores
-        top = jnp.maximum(top, jnp.max(scores, axis=1, keepdims=True))
-
-        def second(number, total):
-            weights = jnp.exp(SCO[:, place(number)] - top)
-            SCO[:, place(number)] = weights
-            return total + jnp.sum(weights, axis=1, keepdims=True)
-
-        total = lax.fori_loop(0, own + 1, second, jnp.zeros((TILE, 1), F32))
-        inverse = 1.0 / total
-
-        def third(number, carried):
-            context, delta = carried
-            probs = SCO[:, place(number)] * inverse
-            value = VH[h, place(number), :]
-            context = context + dot_nn(probs.astype(BF16), value)
-            prob_grad = dot_nt(grad, value)
-            SCO[:, place(number)] = probs
-            DPS[:, place(number)] = prob_grad
-            return context, delta + jnp.sum(probs * prob_grad, axis=1, keepdims=True)
-
-        context, delta = lax.fori_loop(
-            0, own + 1, third, (jnp.zeros((TILE, HD), F32), jnp.zeros((TILE, 1), F32))
-        )
-        CTXH[h, here, :] = context.astype(BF16)
-
-        def fourth(number, query_grad):
-            probs = SCO[:, place(number)]
-            score_grad = (probs * (DPS[:, place(number)] - delta)).astype(BF16)
-            DKT[h, :, place(number)] += dot_nn(query_t, score_grad)
-            DVT[h, :, place(number)] += dot_nn(grad_t, probs.astype(BF16))
-            return query_grad + dot_nn(score_grad, KH[h, place(number), :])
-
-        DQ[h, here, :] = scale * lax.fori_loop(0, own + 1, fourth, jnp.zeros((TILE, HD), F32))
+        for own in range(blocks):
+            pl.when(lax.rem(unit, blocks) == own)(functools.partial(attention_rows, h, own))
 
     def assemble(block):
         base = pl.multiple_of(block * TILE, TILE)
@@ -551,9 +522,8 @@
         base = pl.multiple_of(order(step) * rows, rows)
         here = pl.ds(base, rows)
 
-        @pl.loop(0, width // TILE)
-        def _(part):
-            columns = pl.ds(pl.multiple_of(part * TILE, TILE), TILE)
+        for part in range(width // TILE):
+            columns = slice(part * TILE, (part + 1) * TILE)
             PART[0, here, columns] = (
                 dot_nn(CTX[here, :], WOUT[:, columns]) + dot_nn(HID[here, :], WDN[:, columns])
             ).astype(BF16)
@@ -568,9 +538,8 @@
         spread = jnp.mean((raw - average) * (raw - average), axis=1, keepdims=True)
         inverse_root = lax.rsqrt(spread + epsilon)
 
-        @pl.loop(0, width // TILE)
-        def _(part):
-            columns = pl.ds(pl.multiple_of(part * TILE, TILE), TILE)
+        for part in range(width // TILE):
+            columns = slice(part * TILE, (part + 1) * TILE)
             normed = (T[here, columns].astype(F32) - average) * inverse_root
             attention_back = dot_nt(QG[here, :], WQKV[columns, :])
             feed_back = dot_nt(PG[here, :], WUP[columns, :])
@@ -627,27 +596,31 @@
             spot == 0, sums[0], jnp.where(spot == 1, sums[1], jnp.where(spot == 2, sums[2], 0.0))
         )
 
-    def exchange(step):
-        mate = (
-            core_mate,
-            x_mate,
-            (dp + 1 - 2 * y, t),
-            (2 * (z + 1 - 2 * lax.rem(z, 2)) + y, t),
-            (2 * lax.rem(z + 2, depth) + y, t),
-        )[step]
-        return remote(ES.at[step], EX.at[step], e_s.at[step], e_r.at[step], mate)
-
-    def exchange_send(step):
-        ES[step] = SV[...]
-        exchange(step).start()
-
-    def exchange_receive(step):
-        exchange(step).wait_recv()
-        if step < 2:
+    def share(over, offset):
+        if over == 0:
+            slot, mate = t, (dp, lax.rem(t + offset, 4))
+        else:
+            slot, mate = 4 + dp, (lax.rem(dp + offset, ring), t)
+        return remote(ES.at[over], EX.at[slot], e_s.at[over, offset], e_r.at[over, offset], mate)
+
+    members = (4, ring)
+
+    def share_send(over):
+        ES[over] = SV[...]
+        EX[(4 * over) + (dp if over else t)] = SV[...]
+        for offset in range(1, members[over]):
+            share(over, offset).start()
+
+    def share_receive(over):
+        for offset in range(1, members[over]):
+            share(over, offset).wait_recv()
+        total = EX[4 * over]
+        for number in range(1, members[over]):
+            total = total + EX[4 * over + number]
+        if over == 0:
             row = lax.broadcasted_iota(jnp.int32, SV.shape, 0)
-            SV[...] += jnp.where(row < 6, EX[step], 0.0)
-        else:
-            SV[...] += EX[step]
+            total = jnp.where(row < 6, total, SV[...])
+        SV[...] = total
 
     def chunk(direction, step):
         return lax.rem(at + ring - step, ring) if direction == 0 else lax.rem(at + step, ring)
@@ -668,80 +641,73 @@
                     CTX[:, direction * 128 : (direction + 1) * 128], C[:, columns]
                 )
 
-    def scatter(segment, direction, half, step):
+    def scatter(segment, direction, part, step):
         return remote(
-            RSB.at[segment, direction, half, step], RSB.at[segment, direction, half, step + 1],
-            r_s.at[segment, direction, half, step], r_r.at[segment, direction, half, step], onward[direction],
-        )
-
-    def collect(segment, direction, half, step):
-        piece = GB.at[segment, direction, half, gathered(direction, step)]
+            RSB.at[segment, direction, part, step], RSB.at[segment, direction, part, step + 1],
+            r_s.at[segment, direction, part, step], r_r.at[segment, direction, part, step], onward[direction],
+        )
+
+    def collect(segment, direction, part, step):
+        piece = GB.at[segment, direction, part, gathered(direction, step)]
         sem = ring - 1 + step
         return remote(
             piece, piece,
-            r_s.at[segment, direction, half, sem], r_r.at[segment, direction, half, sem], onward[direction],
-        )
-
-    pieces = [(half, direction) for half in range(2) for direction in range(2)]
+            r_s.at[segment, direction, part, sem], r_r.at[segment, direction, part, sem], onward[direction],
+        )
+
+    pieces = [(part, direction) for part in range(PARTS) for direction in range(2)]
 
     def ring_open(segment):
         own_partial(segment, 0)
-        for half, direction in pieces:
-            RSB[segment, direction, half, 0] = PSC[direction, :, half * 256 : (half + 1) * 256].astype(BF16)
-            scatter(segment, direction, half, 0).start()
+        for part, direction in pieces:
+            RSB[segment, direction, part, 0] = PSC[direction, :, part * 128 : (part + 1) * 128].astype(BF16)
+            scatter(segment, direction, part, 0).start()
 
     def ring_scatter(segment, step):
-        for half, direction in pieces:
-            scatter(segment, direction, half, step - 1).wait_recv()
-            RSB[segment, direction, half, step] = (
-                RSB[segment, direction, half, step].astype(F32)
-                + PSC[direction, :, half * 256 : (half + 1) * 256]
+        for part, direction in pieces:
+            scatter(segment, direction, part, step - 1).wait_recv()
+            RSB[segment, direction, part, step] = (
+                RSB[segment, direction, part, step].astype(F32)
+                + PSC[direction, :, part * 128 : (part + 1) * 128]
             ).astype(BF16)
-            scatter(segment, direction, half, step).start()
+            scatter(segment, direction, part, step).start()
 
     def ring_turn(segment):
         last = ring - 1
-        for half, direction in pieces:
-            scatter(segment, direction, half, last - 1).wait_recv()
-            GB[segment, direction, half, gathered(direction, 0)] = (
-                RSB[segment, direction, half, last].astype(F32)
-                + PSC[direction, :, half * 256 : (half + 1) * 256]
+        for part, direction in pieces:
+            scatter(segment, direction, part, last - 1).wait_recv()
+            GB[segment, direction, part, gathered(direction, 0)] = (
+                RSB[segment, direction, part, last].astype(F32)
+                + PSC[direction, :, part * 128 : (part + 1) * 128]
             ).astype(BF16)
-            collect(segment, direction, half, 0).start()
+            collect(segment, direction, part, 0).start()
 
     def ring_collect(segment, step):
-        for half, direction in pieces:
-            collect(segment, direction, half, step - 1).wait_recv()
-            collect(segment, direction, half, step).start()
+        for part, direction in pieces:
+            collect(segment, direction, part, step - 1).wait_recv()
+            collect(segment, direction, part, step).start()
 
     def ring_close(segment):
-        for half, direction in pieces:
-            collect(segment, direction, half, ring - 2).wait_recv()
-
-    def out_copies(segment, direction, half, number):
-        piece = GB.at[segment, direction, half, number]
+        for part, direction in pieces:
+            collect(segment, direction, part, ring - 2).wait_recv()
+
+    def out_copy(segment, direction, part, number):
         there = pl.ds(number * 128, 128)
-        sem = o_s.at[segment, direction, half, number]
         if segment < 2:
-            out = gd_o if segment == 0 else gu_o
-            return [pltpu.make_async_copy(piece, out.at[there, pl.ds(direction * 512 + half * 256, 256)], sem)]
-        if half == 0:
-            return [pltpu.make_async_copy(piece, gq_o.at[there, pl.ds(direction * 384, 256)], sem)]
-        return [
-            pltpu.make_async_copy(
-                piece.at[:, pl.ds(0, 128)], gq_o.at[there, pl.ds(direction * 384 + 256, 128)], sem
-            ),
-            pltpu.make_async_copy(
-                piece.at[:, pl.ds(128, 128)], go_o.at[pl.ds(direction * 128, 128), there], p_s.at[direction, number]
-            ),
-        ]
+            out = (gd_o if segment == 0 else gu_o).at[there, pl.ds(direction * 512 + part * 128, 128)]
+        elif part < 3:
+            out = gq_o.at[there, pl.ds(direction * 384 + part * 128, 128)]
+        else:
+            out = go_o.at[pl.ds(direction * 128, 128), there]
+        return pltpu.make_async_copy(
+            GB.at[segment, direction, part, number], out, o_s.at[segment, direction, part, number]
+        )
 
     def ring_out(segment, action):
         @pl.loop(0, ring)
         def _(number):
-            for half, direction in pieces:
-                for copy in out_copies(segment, direction, half, number):
-                    getattr(copy, action)()
+            for part, direction in pieces:
+                getattr(out_copy(segment, direction, part, number), action)()
 
     local[0].wait()
     local[2].wait()
@@ -759,9 +725,6 @@
             gather(0, 3).start()
             gather(0, 2).wait_recv()
             gather(0, 4).start()
-            gather(1, 1).start()
-            gather(1, 2).start()
-            gather(1, 0).start()
 
         @pl.when(step == 3)
         def _():
@@ -773,8 +736,13 @@
     local[1].wait()
     local[4].wait()
     local[5].wait()
+
+    def place_of(step):
+        return 2 * lax.rem(x + lax.div(step, 2), 2) + lax.rem(core + lax.rem(step, 2), 2)
+
     gather(1, 1).wait_recv()
     gather(1, 3).start()
+    cotangent_block(place_of(0))
     gather(1, 0).wait_recv()
     gather(1, 2).wait_recv()
     gather(1, 4).start()
@@ -788,69 +756,93 @@
 
     ring_open(0)
 
+    @pl.loop(1, 4)
+    def _(step):
+        cotangent_block(place_of(step))
+
+    ring_open(1)
+
     @pl.loop(1, turns)
     def _(step):
-        own_partial(0, step)
-        during(step <= 4, lambda: cotangent_block(step - 1))
-        during(step > 4, lambda: attention_unit(step - 5))
-        ring_scatter(0, step)
-
-    own_partial(0, turns)
-    ring_turn(0)
+        for segment in range(2):
+            own_partial(segment, step)
+            ring_scatter(segment, step)
+
+        @pl.loop(2 * step - 2, 2 * step)
+        def _(unit):
+            attention_unit(unit)
+
+    for segment in range(2):
+        own_partial(segment, turns)
+        ring_turn(segment)
+
+    @pl.loop(1, 3)
+    def _(step):
+        @pl.loop(2 * step + 10, 2 * step + 12)
+        def _(unit):
+            attention_unit(unit)
+
+        for segment in range(2):
+            ring_collect(segment, step)
+
+    @pl.loop(0, blocks)
+    def _(block):
+        assemble(block)
+
+    ring_open(2)
+
+    @pl.loop(3, turns)
+    def _(step):
+        for segment in range(2):
+            ring_collect(segment, step)
+        own_partial(2, step - 2)
+        ring_scatter(2, step - 2)
+
+        @pl.when(step <= 4)
+        def _():
+            @pl.loop(2 * step - 6, 2 * step - 4)
+            def _(number):
+                back_block(number)
+
+        @pl.when(step == 5)
+        def _():
+            @pl.loop(0, 4)
+            def _(number):
+                branch_block(number)
+
+            chip_sum(1)
+
+        during(step == 6, lambda: chip_sum(0))
+
+    for segment in range(2):
+        ring_close(segment)
+        ring_out(segment, "start")
+
+    @pl.loop(5, turns)
+    def _(step):
+        own_partial(2, step)
+        ring_scatter(2, step)
+
+    own_partial(2, turns)
+    ring_turn(2)
 
     @pl.loop(1, turns)
     def _(step):
-        attention_unit(step + 1)
-        ring_collect(0, step)
-
-    ring_open(1)
-    ring_close(0)
-    ring_out(0, "start")
-
-    @pl.loop(1, turns)
-    def _(step):
-        own_partial(1, step)
-        attention_unit(step + 7)
-        ring_scatter(1, step)
-
-    own_partial(1, turns)
-    ring_turn(1)
-
-    @pl.loop(1, turns)
-    def _(step):
-        during(step <= 2, lambda: attention_unit(step + 13))
-        during(step > 2, lambda: assemble(step - 3))
-        ring_collect(1, step)
-
-    ring_open(2)
-    ring_close(1)
-    ring_out(1, "start")
-
-    @pl.loop(1, turns)
-    def _(step):
-        own_partial(2, step)
-        during(step <= 4, lambda: branch_block(step - 1))
-        during(step > 4, lambda: back_block(step - 5))
-        during(step == 6, lambda: chip_sum(0))
-        ring_scatter(2, step)
-
-    own_partial(2, turns)
-    ring_turn(2)
-
-    @pl.loop(1, turns)
-    def _(step):
-        during(step <= 2, lambda: back_block(step + 1))
-        during(step == 3, lambda: chip_sum(1))
-        during(step == 6, finish)
         ring_collect(2, step)
 
-    exchange_send(0)
+        @pl.when(step == 3)
+        def _():
+            finish()
+            share_send(0)
+
+        @pl.when(step == 5)
+        def _():
+            share_receive(0)
+            share_send(1)
+
     ring_close(2)
     ring_out(2, "start")
-    exchange_receive(0)
-    for step in range(1, 5):
-        exchange_send(step)
-        exchange_receive(step)
+    share_receive(1)
     sv_o[...] = SV[...]
 
     for which in range(2):
@@ -859,15 +851,16 @@
         for slot in range(2):
             to_core(which, slot).wait_send()
         to_x(which).wait_send()
-    for step in range(5):
-        exchange(step).wait_send()
+    for over in range(2):
+        for offset in range(1, members[over]):
+            share(over, offset).wait_send()
     for segment in range(3):
 
         @pl.loop(0, ring - 1)
         def _(step):
-            for half, direction in pieces:
-                scatter(segment, direction, half, step).wait_send()
-                collect(segment, direction, half, step).wait_send()
+            for part, direction in pieces:
+                scatter(segment, direction, part, step).wait_send()
+                collect(segment, direction, part, step).wait_send()
 
         ring_out(segment, "wait")
 
@@ -904,15 +897,14 @@
         V((heads, seq, HD), BF16), V((heads, seq, HD), BF16), V((heads, seq, HD), BF16),
         V((heads, seq, HD), BF16), V((heads, seq, HD), BF16), V((seq, heads * HD), BF16),
         V((heads, seq, HD), F32), V((heads, HD, seq), F32), V((heads, HD, seq), F32),
-        V((TILE, seq), F32), V((TILE, seq), F32),
         V((seq, 128), F32), V((seq, 128), F32),
         V(qkv_weight.shape, BF16), V(out_weight.shape, BF16), V(up_weight.shape, BF16), V(down_weight.shape, BF16),
-        V((3, 2, 2, ring, 128, 256), BF16), V((3, 2, 2, ring, 128, 256), BF16), V((2, 128, 512), F32),
+        V((3, 2, PARTS, ring, 128, 128), BF16), V((3, 2, PARTS, ring, 128, 128), BF16), V((2, 128, 512), F32),
         V((2, seq, width), BF16), V((2, 2, rows, width), BF16), V((2, rows, width), BF16),
-        V((8, width), F32), V((5, 8, width), F32), V((5, 8, width), F32),
+        V((8, width), F32), V((2, 8, width), F32), V((4 + ring, 8, width), F32),
         D((6,)), D((2, 5)), D((2, 5)),
-        D((3, 2, 2, 2 * ring - 2)), D((3, 2, 2, 2 * ring - 2)),
-        D((2, 3)), D((2, 3)), D((5,)), D((5,)), D((3, 2, 2, ring)), D((2, ring)),
+        D((3, 2, PARTS, 2 * ring - 2)), D((3, 2, PARTS, 2 * ring - 2)),
+        D((2, 3)), D((2, 3)), D((2, ring)), D((2, ring)), D((3, 2, PARTS, ring)),
     ]
     mixed, input_grad, gd, gu, gq, go, sv = pl.pallas_call(
         functools.partial(fused_kernel, ring),
@@ -936,12 +928,59 @@
         qkv_weight, out_weight, up_weight, down_weight, cos_a, sin_a, cos_b, sin_b,
     )
     elements = rows * width * ring * lax.axis_size("tensor")
-    statistics = jnp.sqrt(sv[5, :3] / elements)
-    return (
-        mixed, input_grad, sv[0], sv[1], sv[2], sv[3],
-        gq.astype(F32), sv[7, :qkv_width], go.astype(F32), sv[4],
-        gu.astype(F32), sv[6], gd.astype(F32), sv[4], statistics,
-    )
+    return export_outputs(mixed, input_grad, gd, gu, gq, go, sv, elements)
+
+
+def export_kernel(
+    elements,
+    mixed, igrad, gd, gu, gq, go, sv,
+    mixed_o, igrad_o, ga_o, ba_o, gm_o, bm_o, gq_o, bqkv_o, go_o, bo_o, gu_o, bup_o, gd_o, bd_o, stats_o,
+):
+    @pl.when(pl.program_id(0) == 0)
+    def _():
+        for row, out in enumerate((ga_o, ba_o, gm_o, bm_o, bo_o)):
+            out[...] = sv[row : row + 1, :]
+        bd_o[...] = sv[4:5, :]
+        bup_o[...] = sv[6:7, :]
+        bqkv_o[...] = sv[7, : bqkv_o.shape[0]]
+        stats_o[...] = jnp.sqrt(sv[5, : stats_o.shape[0]] * (1.0 / elements))
+
+    for source, out in ((gd, gd_o), (gu, gu_o), (gq, gq_o), (go, go_o), (mixed, mixed_o), (igrad, igrad_o)):
+        out[...] = source[...].astype(out.dtype)
+
+
+def export_outputs(mixed, input_grad, gd, gu, gq, go, sv, elements):
+    steps = 4
+
+    def tiled(array):
+        return pl.BlockSpec((array.shape[0] // steps, array.shape[1]), lambda i: (i, 0))
+
+    def whole(*shape):
+        return pl.BlockSpec(shape, lambda i: (0,) * len(shape))
+
+    def like(array, dtype=F32):
+        return jax.ShapeDtypeStruct(array.shape, dtype)
+
+    width = sv.shape[1]
+    row = jax.ShapeDtypeStruct((1, width), F32)
+    row_spec = whole(1, width)
+    qkv_width = gq.shape[1]
+    outs = pl.pallas_call(
+        functools.partial(export_kernel, elements),
+        grid=(steps,),
+        in_specs=[tiled(mixed), tiled(input_grad), tiled(gd), tiled(gu), tiled(gq), tiled(go), whole(*sv.shape)],
+        out_specs=[
+            tiled(mixed), tiled(input_grad), row_spec, row_spec, row_spec, row_spec, tiled(gq), whole(qkv_width), tiled(go), row_spec,
+            tiled(gu), row_spec, tiled(gd), row_spec, whole(3),
+        ],
+        out_shape=[
+            like(mixed, BF16), like(input_grad), row, row, row, row, like(gq), jax.ShapeDtypeStruct((qkv_width,), F32),
+            like(go), row, like(gu), row, like(gd), row, jax.ShapeDtypeStruct((3,), F32),
+        ],
+        compiler_params=pltpu.CompilerParams(vmem_limit_bytes=VMEM_LIMIT),
+        name="outputs",
+    )(mixed, input_grad, gd, gu, gq, go, sv)
+    return tuple(out.reshape(-1) if out.shape == (1, width) else out for out in outs)
 
 
 def solution(mesh):

time: 235 us -> 189 us (0.80)
  Pallas kernels: 216 us -> 186 us
  other arithmetic: 10.9 us -> 0 us
  local copies, waits for them, and re-layouts: 6.59 us -> 1.27 us
    pallas_call x1, Pallas kernels: 216 us -> 177 us  [per_device_fused(): pl.pallas_call(functools.partial(fused_kernel, ring), out_shape=[jax.Shap...]
    convert_element_type x4 -> x0, other arithmetic: 9.68 us -> none  [the longest x1 4.22 us: per_device_fused(): gu.astype(F32)]
    pallas_call x0 -> x1, Pallas kernels: none -> 9.05 us  [export_outputs(): pl.pallas_call(functools.partial(export_kernel, elements), grid=(steps,),...]
    slice x2 -> x0, local copies, waits for them, and re-layouts: 2.94 us -> none  [the longest x1 1.6 us: per_device_fused(): sv[6]]
    unnamed x15 -> x0, local copies, waits for them, and re-layouts: 2.38 us -> none
where the time goes in v2:
time: 189 us
  Pallas kernels  186 us (98%)
    pallas_call x1, Pallas kernels, per_device_fused(): pl.pallas_call(functools.partial(fused_kernel, ring), out_shape=[jax.Shap...  177 us
    pallas_call x1, Pallas kernels, export_outputs(): pl.pallas_call(functools.partial(export_kernel, elements), grid=(steps,),...  9.05 us

profile of v2, /device:TPU:0, one launch (start us, length us, event | category | flops | bytes accessed | tf_op | source)
XLA Modules:
  0.0 188.5 jit_solution(1317812735629754224)
XLA Ops:
  0.6 1.3 reshape.81.bqkv
  1.9 177.4 %layer.1 = (bf16[256,1024]{1,0:T(8,128)(2,1)}, f32[256,1024]{1,0:T(8,128)}, bf16[1024,1024]{1,0:T(8,128)(2,1)}, bf16[1024,1024]{1,0:T(8,128)(2,1)}, bf16[1024,76...) custom-call(bf16[256,1024]{1,0:T(8,128)(2,1)} %tok.1, bf16[256,1024]{1,0:T(8,128)(2,1)} %cot.1, ...), custom_call_target="tpu_custom_call" | custom-call | tf_op jit(solution)/shard_map/layer/pallas_call | solution.py:909
  179.3 9.0 %outputs.1 = (bf16[256,1024]{1,0:T(8,128)(2,1)}, f32[256,1024]{1,0:T(8,128)}, f32[1,1024]{1,0:T(1,128)}, f32[1,1024]{1,0:T(1,128)}, f32[1,1024]{1,0:T(1,128)}, /...) custom-call(bf16[256,1024]{1,0:T(8,128)(2,1)} %get-tuple-element.37., ...), custom_call_target="tpu_custom_call" | custom-call | tf_op jit(solution)/shard_map/outputs/pallas_call | solution.py:968

commit v3 on v2

--- a/solution.py
+++ b/solution.py
@@ -11,7 +11,7 @@
 
 HD = 64
 ROT = 16
-VMEM_LIMIT = 62 << 20
+VMEM_LIMIT = 54 << 20
 
 
 epsilon = 1e-05
@@ -286,10 +286,10 @@
 def fused_kernel(
     ring,
     tok, cot, ga, ba, gm, bm, bo, bd, bqkv, bup, wqkv_h, wout_h, wup_h, wdn_h, cos_a, sin_a, cos_b, sin_b,
-    mixed, igrad, gd_o, gu_o, gq_o, go_o, sv_o,
+    mixed, igrad, GB, SV,
     T, C, AI, FI, HID, GP, PG, QG, QH, KH, VH, CGH, CTXH, CTX, DQ, DKT, DVT, COS, SIN,
-    WQKV, WOUT, WUP, WDN, RSB, GB, PSC, PART, RA, RB, SV, ES, EX,
-    lsem, g_s, g_r, r_s, r_r, b_s, b_r, e_s, e_r, o_s,
+    WQKV, WOUT, WUP, WDN, RSB, PSC, PART, RA, RB, ES, EX,
+    lsem, g_s, g_r, r_s, r_r, b_s, b_r, e_s, e_r,
 ):
     rows = tok.shape[0]
     width = tok.shape[1]
@@ -339,20 +339,24 @@
 
     local = [
         pltpu.make_async_copy(tok, T.at[pl.ds(t * rows, rows)], lsem.at[0]),
-        pltpu.make_async_copy(cot, C.at[pl.ds(t * rows, rows)], lsem.at[1]),
         pltpu.make_async_copy(wqkv_h, WQKV, lsem.at[2]),
         pltpu.make_async_copy(wup_h, WUP, lsem.at[3]),
+        pltpu.make_async_copy(cot, C.at[pl.ds(t * rows, rows)], lsem.at[1]),
         pltpu.make_async_copy(wdn_h, WDN, lsem.at[4]),
         pltpu.make_async_copy(wout_h, WOUT, lsem.at[5]),
     ]
+    for copy in local:
+        copy.start()
+    barrier = pltpu.get_barrier_semaphore()
+    for mate in (core_mate, x_mate, following, previous):
+        pl.semaphore_signal(barrier, inc=1, device_id=mate, device_id_type=MESH)
+    pl.semaphore_wait(barrier, 4)
     gather(0, 1).start()
     gather(0, 2).start()
     gather(0, 0).start()
     gather(1, 1).start()
     gather(1, 2).start()
     gather(1, 0).start()
-    for copy in (local[0], local[2], local[3], local[1], local[4], local[5]):
-        copy.start()
 
     @pl.loop(0, seq // 32)
     def _(a):
@@ -401,7 +405,7 @@
         for group in range(3 * heads // 2):
             if group % 2 == 0:
                 columns = slice(group * 128, group * 128 + 256)
-                pair = dot_nn(AI[pl.ds(base, rows), :], WQKV[:, columns]) + bqkv[:, columns]
+                pair = dot_nn(AI[pl.ds(base, rows), :], WQKV[:, columns]) + bqkv[columns].reshape(1, 256)
             value = pair[:, (group % 2) * 128 : (group % 2) * 128 + 128]
             cosine, upper, lower = tables(base, group % 3)
             turned = (
@@ -691,27 +695,8 @@
         for part, direction in pieces:
             collect(segment, direction, part, ring - 2).wait_recv()
 
-    def out_copy(segment, direction, part, number):
-        there = pl.ds(number * 128, 128)
-        if segment < 2:
-            out = (gd_o if segment == 0 else gu_o).at[there, pl.ds(direction * 512 + part * 128, 128)]
-        elif part < 3:
-            out = gq_o.at[there, pl.ds(direction * 384 + part * 128, 128)]
-        else:
-            out = go_o.at[pl.ds(direction * 128, 128), there]
-        return pltpu.make_async_copy(
-            GB.at[segment, direction, part, number], out, o_s.at[segment, direction, part, number]
-        )
-
-    def ring_out(segment, action):
-        @pl.loop(0, ring)
-        def _(number):
-            for part, direction in pieces:
-                getattr(out_copy(segment, direction, part, number), action)()
-
-    local[0].wait()
-    local[2].wait()
-    local[3].wait()
+    for copy in local[:3]:
+        copy.wait()
 
     @pl.loop(0, 4)
     def _(step):
@@ -733,9 +718,8 @@
 
         forward_block(2 * lax.rem(x + lax.div(step, 2), 2) + lax.rem(core + lax.rem(step, 2), 2))
 
-    local[1].wait()
-    local[4].wait()
-    local[5].wait()
+    for copy in local[3:]:
+        copy.wait()
 
     def place_of(step):
         return 2 * lax.rem(x + lax.div(step, 2), 2) + lax.rem(core + lax.rem(step, 2), 2)
@@ -816,7 +800,6 @@
 
     for segment in range(2):
         ring_close(segment)
-        ring_out(segment, "start")
 
     @pl.loop(5, turns)
     def _(step):
@@ -841,9 +824,7 @@
             share_send(1)
 
     ring_close(2)
-    ring_out(2, "start")
     share_receive(1)
-    sv_o[...] = SV[...]
 
     for which in range(2):
         for kind in range(5):
@@ -861,8 +842,6 @@
             for part, direction in pieces:
                 scatter(segment, direction, part, step).wait_send()
                 collect(segment, direction, part, step).wait_send()
-
-        ring_out(segment, "wait")
 
 
 def angle_parts(seq_len):
@@ -899,87 +878,110 @@
         V((heads, seq, HD), F32), V((heads, HD, seq), F32), V((heads, HD, seq), F32),
         V((seq, 128), F32), V((seq, 128), F32),
         V(qkv_weight.shape, BF16), V(out_weight.shape, BF16), V(up_weight.shape, BF16), V(down_weight.shape, BF16),
-        V((3, 2, PARTS, ring, 128, 128), BF16), V((3, 2, PARTS, ring, 128, 128), BF16), V((2, 128, 512), F32),
+        V((3, 2, PARTS, ring, 128, 128), BF16), V((2, 128, 512), F32),
         V((2, seq, width), BF16), V((2, 2, rows, width), BF16), V((2, rows, width), BF16),
-        V((8, width), F32), V((2, 8, width), F32), V((4 + ring, 8, width), F32),
+        V((2, 8, width), F32), V((4 + ring, 8, width), F32),
         D((6,)), D((2, 5)), D((2, 5)),
         D((3, 2, PARTS, 2 * ring - 2)), D((3, 2, PARTS, 2 * ring - 2)),
-        D((2, 3)), D((2, 3)), D((2, ring)), D((2, ring)), D((3, 2, PARTS, ring)),
+        D((2, 3)), D((2, 3)), D((2, ring)), D((2, ring)),
     ]
-    mixed, input_grad, gd, gu, gq, go, sv = pl.pallas_call(
+    mixed, input_grad, gradients, sums = pl.pallas_call(
         functools.partial(fused_kernel, ring),
         out_shape=[
-            jax.ShapeDtypeStruct((rows, width), BF16),
-            jax.ShapeDtypeStruct((rows, width), F32),
-            jax.ShapeDtypeStruct(down_weight.shape, BF16),
-            jax.ShapeDtypeStruct(up_weight.shape, BF16),
-            jax.ShapeDtypeStruct(qkv_weight.shape, BF16),
-            jax.ShapeDtypeStruct(out_weight.shape, BF16),
-            jax.ShapeDtypeStruct((8, width), F32),
+            V((rows, width), BF16),
+            V((rows, width), F32),
+            V((3, 2, PARTS, ring, 128, 128), BF16),
+            V((8, width), F32),
         ],
         in_specs=[hbm, hbm] + [vmem] * 8 + [hbm] * 4 + [vmem] * 4,
-        out_specs=[vmem, vmem, hbm, hbm, hbm, hbm, vmem],
+        out_specs=[vmem] * 4,
         scratch_shapes=scratch,
-        compiler_params=pltpu.CompilerParams(has_side_effects=True, vmem_limit_bytes=VMEM_LIMIT),
+        compiler_params=pltpu.CompilerParams(
+            collective_id=0, has_side_effects=True, vmem_limit_bytes=VMEM_LIMIT
+        ),
         name="layer",
     )(
         tokens, cotangent,
-        *(v.reshape(1, -1) for v in (gain_attn, bias_attn, gain_mlp, bias_mlp, out_bias, down_bias, qkv_bias, up_bias)),
+        *(v.reshape(1, -1) for v in (gain_attn, bias_attn, gain_mlp, bias_mlp, out_bias, down_bias)),
+        qkv_bias, up_bias.reshape(1, -1),
         qkv_weight, out_weight, up_weight, down_weight, cos_a, sin_a, cos_b, sin_b,
     )
     elements = rows * width * ring * lax.axis_size("tensor")
-    return export_outputs(mixed, input_grad, gd, gu, gq, go, sv, elements)
-
-
-def export_kernel(
+    return closing(mixed, input_grad, gradients, sums, elements, down_weight, up_weight, qkv_weight, out_weight)
+
+
+def closing_kernel(
     elements,
-    mixed, igrad, gd, gu, gq, go, sv,
+    mixed, igrad, GB, SV,
     mixed_o, igrad_o, ga_o, ba_o, gm_o, bm_o, gq_o, bqkv_o, go_o, bo_o, gu_o, bup_o, gd_o, bd_o, stats_o,
+    SD, SU, SQ, SO, sems, msem,
 ):
-    @pl.when(pl.program_id(0) == 0)
-    def _():
-        for row, out in enumerate((ga_o, ba_o, gm_o, bm_o, bo_o)):
-            out[...] = sv[row : row + 1, :]
-        bd_o[...] = sv[4:5, :]
-        bup_o[...] = sv[6:7, :]
-        bqkv_o[...] = sv[7, : bqkv_o.shape[0]]
-        stats_o[...] = jnp.sqrt(sv[5, : stats_o.shape[0]] * (1.0 / elements))
-
-    for source, out in ((gd, gd_o), (gu, gu_o), (gq, gq_o), (go, go_o), (mixed, mixed_o), (igrad, igrad_o)):
-        out[...] = source[...].astype(out.dtype)
-
-
-def export_outputs(mixed, input_grad, gd, gu, gq, go, sv, elements):
-    steps = 4
-
-    def tiled(array):
-        return pl.BlockSpec((array.shape[0] // steps, array.shape[1]), lambda i: (i, 0))
-
-    def whole(*shape):
-        return pl.BlockSpec(shape, lambda i: (0,) * len(shape))
+    copies = [
+        pltpu.make_async_copy(mixed, mixed_o, msem.at[0]),
+        pltpu.make_async_copy(igrad, igrad_o, msem.at[1]),
+    ]
+    for copy in copies:
+        copy.start()
+    for segment, stage in enumerate((SD, SU, SQ)):
+        for number in range(GB.shape[3]):
+            there = slice(number * 128, number * 128 + 128)
+            for direction in range(2):
+                for part in range(PARTS):
+                    piece = GB[segment, direction, part, number].astype(F32)
+                    if segment == 2 and part == 3:
+                        SO[direction * 128 : direction * 128 + 128, there] = piece
+                    else:
+                        column = direction * (384 if segment == 2 else 512) + part * 128
+                        stage[there, column : column + 128] = piece
+            rows = pl.ds(number * 128, 128)
+            copy = pltpu.make_async_copy(
+                stage.at[rows], (gd_o, gu_o, gq_o)[segment].at[rows], sems.at[segment, number]
+            )
+            copy.start()
+            copies.append(copy)
+    copies.append(pltpu.make_async_copy(SO, go_o, msem.at[2]))
+    copies[-1].start()
+    for row, out in enumerate((ga_o, ba_o, gm_o, bm_o, bo_o)):
+        out[...] = SV[row : row + 1, :]
+    bd_o[...] = SV[4:5, :]
+    bup_o[...] = SV[6:7, :]
+    bqkv_o[...] = SV[7, : bqkv_o.shape[0]]
+    stats_o[...] = jnp.sqrt(SV[5, : stats_o.shape[0]] * (1.0 / elements))
+    for copy in copies:
+        copy.wait()
+
+
+def closing(mixed, input_grad, gradients, sums, elements, down_weight, up_weight, qkv_weight, out_weight):
+    hbm = pl.BlockSpec(memory_space=pl.ANY)
+    vmem = pl.BlockSpec(memory_space=pltpu.VMEM)
 
     def like(array, dtype=F32):
         return jax.ShapeDtypeStruct(array.shape, dtype)
 
-    width = sv.shape[1]
+    width = sums.shape[1]
     row = jax.ShapeDtypeStruct((1, width), F32)
-    row_spec = whole(1, width)
-    qkv_width = gq.shape[1]
     outs = pl.pallas_call(
-        functools.partial(export_kernel, elements),
-        grid=(steps,),
-        in_specs=[tiled(mixed), tiled(input_grad), tiled(gd), tiled(gu), tiled(gq), tiled(go), whole(*sv.shape)],
+        functools.partial(closing_kernel, elements),
+        in_specs=[vmem] * 4,
         out_specs=[
-            tiled(mixed), tiled(input_grad), row_spec, row_spec, row_spec, row_spec, tiled(gq), whole(qkv_width), tiled(go), row_spec,
-            tiled(gu), row_spec, tiled(gd), row_spec, whole(3),
+            hbm, hbm, vmem, vmem, vmem, vmem, hbm, vmem, hbm, vmem, hbm, vmem, hbm, vmem, vmem,
         ],
         out_shape=[
-            like(mixed, BF16), like(input_grad), row, row, row, row, like(gq), jax.ShapeDtypeStruct((qkv_width,), F32),
-            like(go), row, like(gu), row, like(gd), row, jax.ShapeDtypeStruct((3,), F32),
+            like(mixed, BF16), like(input_grad), row, row, row, row,
+            like(qkv_weight), jax.ShapeDtypeStruct((qkv_weight.shape[1],), F32), like(out_weight), row,
+            like(up_weight), row, like(down_weight), row, jax.ShapeDtypeStruct((3,), F32),
         ],
-        compiler_params=pltpu.CompilerParams(vmem_limit_bytes=VMEM_LIMIT),
+        scratch_shapes=[
+            pltpu.VMEM(down_weight.shape, F32),
+            pltpu.VMEM(up_weight.shape, F32),
+            pltpu.VMEM(qkv_weight.shape, F32),
+            pltpu.VMEM(out_weight.shape, F32),
+            pltpu.SemaphoreType.DMA((3, gradients.shape[3])),
+            pltpu.SemaphoreType.DMA((3,)),
+        ],
+        compiler_params=pltpu.CompilerParams(vmem_limit_bytes=24 << 20),
         name="outputs",
-    )(mixed, input_grad, gd, gu, gq, go, sv)
+    )(mixed, input_grad, gradients, sums)
     return tuple(out.reshape(-1) if out.shape == (1, width) else out for out in outs)
 
 

time: 189 us -> 174 us (0.921)
  Pallas kernels: 186 us -> 173 us
    pallas_call x2, Pallas kernels: 186 us -> 173 us  [the longest x1 167 us: per_device_fused(): pl.pallas_call(functools.partial(fused_kernel, ring), out_shape=[V((rows,...]
where the time goes in v3:
time: 174 us
  Pallas kernels  173 us (99%)
    pallas_call x1, Pallas kernels, per_device_fused(): pl.pallas_call(functools.partial(fused_kernel, ring), out_shape=[V((rows,...  167 us
    pallas_call x1, Pallas kernels, closing(): pl.pallas_call(functools.partial(closing_kernel, elements), in_specs=[vme...  5.95 us

profile of v3, /device:TPU:0, one launch (start us, length us, event | category | flops | bytes accessed | tf_op | source)
XLA Modules:
  0.0 174.1 jit_solution(1236959242892469736)
XLA Ops:
  0.7 167.3 %layer.1 = (bf16[256,1024]{1,0:T(8,128)(2,1)S(1)}, f32[256,1024]{1,0:T(8,128)S(1)}, bf16[3,2,4,8,128,128]{5,4,3,2,1,0:T(8,128)(2,1)S(1)}, f32[8,1024]{1,0:T(8,128)S(1)}) custom-call(bf16[256,1024]{1,0:T(8,128)(2,1)} %tok.1, bf16[256,1024]{1,0:T(8,128)(2,1)} %cot.1, f32[1,1024]{1,0:T(1,128)} %bitcast.14, f32[1,1024]{1,0:T(1,128)} %bitcast.15, ...), custom_call_target="tpu_custom_call" | custom-call | tf_op jit(solution)/shard_map/layer/pallas_call | solution.py:888
  168.0 5.9 %outputs.1 = (bf16[256,1024]{1,0:T(8,128)(2,1)}, f32[256,1024]{1,0:T(8,128)}, f32[1,1024]{1,0:T(1,128)}, f32[1,1024]{1,0:T(1,128)}, f32[1,1024]{1,0:T(1,128)}, /...) custom-call(bf16[256,1024]{1,0:T(8,128)(2,1)S(1)} %get-tuple-element, ...), custom_call_target="tpu_custom_call" | custom-call | tf_op jit(solution)/shard_map/outputs/pallas_call | solution.py:963

commit v4 on v3

--- a/solution.py
+++ b/solution.py
@@ -269,6 +269,7 @@
 MESH = pl.DeviceIdType.MESH
 TILE = 256
 PARTS = 4
+TOGETHER = (1, 2, 1)
 
 
 def dot_nn(left, right):
@@ -286,9 +287,9 @@
 def fused_kernel(
     ring,
     tok, cot, ga, ba, gm, bm, bo, bd, bqkv, bup, wqkv_h, wout_h, wup_h, wdn_h, cos_a, sin_a, cos_b, sin_b,
-    mixed, igrad, GB, SV,
-    T, C, AI, FI, HID, GP, PG, QG, QH, KH, VH, CGH, CTXH, CTX, DQ, DKT, DVT, COS, SIN,
-    WQKV, WOUT, WUP, WDN, RSB, PSC, PART, RA, RB, ES, EX,
+    mixed, igrad, GB, SUMS, SQO,
+    T, CB, AI, FI, HID, GP, PG, QG, QH, KH, VH, CGH, CTXH, CTX, DQ, DKT, DVT, COS, SIN,
+    WQKV, WOUT, WUP, WDN, RSB, PSD, PSC, PART, RA, RB, SV, ES, EX, EROWS, EY, SQ, EQ, EZ,
     lsem, g_s, g_r, r_s, r_r, b_s, b_r, e_s, e_r,
 ):
     rows = tok.shape[0]
@@ -325,23 +326,42 @@
         )
 
     def gather(which, kind):
-        src, full = (tok, T) if which == 0 else (cot, C)
         sems = (g_s.at[which, kind], g_r.at[which, kind])
+        own = pl.ds(t * rows, rows)
+        there = pl.ds(x_block * rows, rows)
+        if which == 1:
+            if kind == 0:
+                return remote(CB.at[:, :, own], CB.at[:, :, own], *sems, core_mate)
+            if kind <= PARTS:
+                return remote(CB.at[kind - 1, :, own], CB.at[kind - 1, :, own], *sems, x_mate)
+            piece = CB.at[kind - 1 - PARTS, :, there]
+            return remote(piece, piece, *sems, core_mate)
         if kind == 0:
-            return remote(src, full.at[pl.ds(t * rows, rows)], *sems, core_mate)
+            return remote(tok, T.at[own], *sems, core_mate)
         if kind <= 2:
             off = (kind - 1) * half_rows
-            return remote(
-                src.at[pl.ds(off, half_rows)], full.at[pl.ds(t * rows + off, half_rows)], *sems, x_mate
-            )
-        part = full.at[pl.ds(x_block * rows + (kind - 3) * half_rows, half_rows)]
+            return remote(tok.at[pl.ds(off, half_rows)], T.at[pl.ds(t * rows + off, half_rows)], *sems, x_mate)
+        part = T.at[pl.ds(x_block * rows + (kind - 3) * half_rows, half_rows)]
         return remote(part, part, *sems, core_mate)
+
+    kinds = (5, 1 + 2 * PARTS)
+
+    def upstream_rows(here):
+        return jnp.concatenate([CB[part, direction, here, :] for direction in range(2) for part in range(PARTS)], axis=1)
 
     local = [
         pltpu.make_async_copy(tok, T.at[pl.ds(t * rows, rows)], lsem.at[0]),
         pltpu.make_async_copy(wqkv_h, WQKV, lsem.at[2]),
         pltpu.make_async_copy(wup_h, WUP, lsem.at[3]),
-        pltpu.make_async_copy(cot, C.at[pl.ds(t * rows, rows)], lsem.at[1]),
+        *(
+            pltpu.make_async_copy(
+                cot.at[:, pl.ds(direction * 512 + part * 128, 128)],
+                CB.at[part, direction, pl.ds(t * rows, rows)],
+                lsem.at[6 + 2 * part + direction],
+            )
+            for part in range(PARTS)
+            for direction in range(2)
+        ),
         pltpu.make_async_copy(wdn_h, WDN, lsem.at[4]),
         pltpu.make_async_copy(wout_h, WOUT, lsem.at[5]),
     ]
@@ -354,9 +374,6 @@
     gather(0, 1).start()
     gather(0, 2).start()
     gather(0, 0).start()
-    gather(1, 1).start()
-    gather(1, 2).start()
-    gather(1, 0).start()
 
     @pl.loop(0, seq // 32)
     def _(a):
@@ -366,17 +383,18 @@
         SIN[pl.ds(a * 32, 32), :] = sa * cb + ca * sb
 
     SV[...] = jnp.zeros_like(SV)
+    SQ[...] = jnp.zeros_like(SQ)
 
     @pl.loop(0, heads)
     def _(h):
         DKT[h] = jnp.zeros(DKT.shape[1:], F32)
         DVT[h] = jnp.zeros(DVT.shape[1:], F32)
 
-    lane = lax.broadcasted_iota(jnp.int32, (TILE, 128), 1)
-    low_lane = jnp.where(lane >= 64, lane - 64, lane)
-
-    def tables(base, group):
-        cosine, sine = COS[pl.ds(base, TILE), :], SIN[pl.ds(base, TILE), :]
+
+    def tables(base, group, count):
+        lane = lax.broadcasted_iota(jnp.int32, (count, 128), 1)
+        low_lane = jnp.where(lane >= 64, lane - 64, lane)
+        cosine, sine = COS[pl.ds(base, count), :], SIN[pl.ds(base, count), :]
         if group == 1:
             cosine = jnp.where(lane >= 64, cosine, 1.0)
             sine = jnp.where(lane >= 64, sine, 0.0)
@@ -392,10 +410,10 @@
         inverse_root = lax.rsqrt(jnp.mean(centred * centred, axis=1, keepdims=True) + epsilon)
         return centred * inverse_root, inverse_root
 
-    def forward_block(block):
-        base = pl.multiple_of(block * rows, rows)
-
-        @pl.loop(0, rows // 64)
+    def forward_block(block, half):
+        base = pl.multiple_of(block * rows + half * half_rows, half_rows)
+
+        @pl.loop(0, half_rows // 64)
         def _(part):
             off = pl.multiple_of(base + part * 64, 64)
             normed, _ = norm_rows(off, 64)
@@ -405,9 +423,9 @@
         for group in range(3 * heads // 2):
             if group % 2 == 0:
                 columns = slice(group * 128, group * 128 + 256)
-                pair = dot_nn(AI[pl.ds(base, rows), :], WQKV[:, columns]) + bqkv[columns].reshape(1, 256)
+                pair = dot_nn(AI[pl.ds(base, half_rows), :], WQKV[:, columns]) + bqkv[columns].reshape(1, 256)
             value = pair[:, (group % 2) * 128 : (group % 2) * 128 + 128]
-            cosine, upper, lower = tables(base, group % 3)
+            cosine, upper, lower = tables(base, group % 3, half_rows)
             turned = (
                 value * cosine
                 - lower * pltpu.roll(value, 128 - ROT // 2, 1)
@@ -416,20 +434,20 @@
             first = 2 * (group // 3)
             left, left_head = ((QH, first), (VH, first), (KH, first + 1))[group % 3]
             right, right_head = ((KH, first), (QH, first + 1), (VH, first + 1))[group % 3]
-            left[left_head, pl.ds(base, rows), :] = turned[:, :HD]
-            right[right_head, pl.ds(base, rows), :] = turned[:, HD:]
+            left[left_head, pl.ds(base, half_rows), :] = turned[:, :HD]
+            right[right_head, pl.ds(base, half_rows), :] = turned[:, HD:]
 
         for part in range(hidden_width // TILE):
             columns = slice(part * TILE, (part + 1) * TILE)
-            preact = dot_nn(FI[pl.ds(base, rows), :], WUP[:, columns]) + bup[:, columns]
+            preact = dot_nn(FI[pl.ds(base, half_rows), :], WUP[:, columns]) + bup[:, columns]
             cdf = 0.5 * (1.0 + lax.erf(preact * 0.5**0.5))
             density = jnp.exp(-0.5 * preact * preact) * (1.0 / math.sqrt(2.0 * math.pi))
-            HID[pl.ds(base, rows), columns] = (preact * cdf).astype(BF16)
-            GP[pl.ds(base, rows), columns] = cdf + preact * density
+            HID[pl.ds(base, half_rows), columns] = (preact * cdf).astype(BF16)
+            GP[pl.ds(base, half_rows), columns] = cdf + preact * density
 
     def cotangent_block(block):
         base = pl.multiple_of(block * rows, rows)
-        upstream = C[pl.ds(base, rows), :]
+        upstream = upstream_rows(pl.ds(base, rows))
         grad = dot_nt(upstream, WOUT[...]).astype(BF16)
         for h in range(heads):
             CGH[h, pl.ds(base, rows), :] = grad[:, h * HD : (h + 1) * HD]
@@ -467,8 +485,8 @@
 
     def attention_unit(unit):
         h = lax.div(unit, blocks)
-        for own in range(blocks):
-            pl.when(lax.rem(unit, blocks) == own)(functools.partial(attention_rows, h, own))
+        for number, own in enumerate(sorted(range(blocks), key=lambda own: min(own, blocks - 1 - own))):
+            pl.when(lax.rem(unit, blocks) == number)(functools.partial(attention_rows, h, own))
 
     def assemble(block):
         base = pl.multiple_of(block * TILE, TILE)
@@ -485,7 +503,7 @@
             ]
             for group, (left, right) in enumerate(parts):
                 grad = jnp.concatenate([left, right], axis=1)
-                cosine, upper, lower = tables(base, group)
+                cosine, upper, lower = tables(base, group, TILE)
                 turned = (
                     grad * cosine
                     + pltpu.roll(grad * upper, 128 - ROT // 2, 1)
@@ -561,70 +579,102 @@
         PART[which, there, :] = (PART[which, there, :].astype(F32) + RA[which, 1].astype(F32)).astype(BF16)
         to_x(which).start()
 
-    def finish():
+    def finish_start():
         for which in range(2):
             to_core(which, 0).wait_recv()
             to_x(which).wait_recv()
-        SV[4:5, :] = jnp.sum(C[pl.ds(t * rows, rows), :].astype(F32), axis=0, keepdims=True)
-
-        def total(which, off):
-            return (
-                PART[which, pl.ds(pl.multiple_of(t * rows + off, 64), 64), :].astype(F32)
-                + RA[which, 0, pl.ds(off, 64), :].astype(F32)
-                + RB[which, pl.ds(off, 64), :].astype(F32)
-            )
-
-        def square(value):
-            return jnp.sum(jnp.sum(value * value, axis=1, keepdims=True), axis=0, keepdims=True)
-
-        def part(number, sums):
-            off = pl.multiple_of(number * 64, 64)
-            here = pl.ds(pl.multiple_of(t * rows + off, 64), 64)
-            branch = total(0, off) + bo[...] + bd[...]
-            residual = T[here, :].astype(F32) + branch
-            mixed[pl.ds(off, 64), :] = residual.astype(BF16)
-            normed, inverse_root = norm_rows(t * rows + off, 64)
-            grad = total(1, off)
-            grad = inverse_root * (
-                grad
-                - jnp.mean(grad, axis=1, keepdims=True)
-                - normed * jnp.mean(grad * normed, axis=1, keepdims=True)
-            ) + C[here, :].astype(F32)
-            igrad[pl.ds(off, 64), :] = grad
-            return sums[0] + square(residual), sums[1] + square(branch), sums[2] + square(grad)
-
-        zero = jnp.zeros((1, 1), F32)
-        sums = lax.fori_loop(0, rows // 64, part, (zero, zero, zero))
-        spot = lax.broadcasted_iota(jnp.int32, (1, width), 1)
-        SV[5:6, :] = jnp.where(
-            spot == 0, sums[0], jnp.where(spot == 1, sums[1], jnp.where(spot == 2, sums[2], 0.0))
-        )
-
-    def share(over, offset):
-        if over == 0:
-            slot, mate = t, (dp, lax.rem(t + offset, 4))
-        else:
-            slot, mate = 4 + dp, (lax.rem(dp + offset, ring), t)
-        return remote(ES.at[over], EX.at[slot], e_s.at[over, offset], e_r.at[over, offset], mate)
-
-    members = (4, ring)
-
-    def share_send(over):
-        ES[over] = SV[...]
-        EX[(4 * over) + (dp if over else t)] = SV[...]
-        for offset in range(1, members[over]):
-            share(over, offset).start()
-
-    def share_receive(over):
-        for offset in range(1, members[over]):
-            share(over, offset).wait_recv()
-        total = EX[4 * over]
-        for number in range(1, members[over]):
-            total = total + EX[4 * over + number]
-        if over == 0:
-            row = lax.broadcasted_iota(jnp.int32, SV.shape, 0)
-            total = jnp.where(row < 6, total, SV[...])
-        SV[...] = total
+    def total(which, off):
+        return (
+            PART[which, pl.ds(pl.multiple_of(t * rows + off, 64), 64), :].astype(F32)
+            + RA[which, 0, pl.ds(off, 64), :].astype(F32)
+            + RB[which, pl.ds(off, 64), :].astype(F32)
+        )
+
+    def square(value):
+        return jnp.sum(jnp.sum(value * value, axis=1, keepdims=True), axis=0, keepdims=True)
+
+    def finish_part(number):
+        off = pl.multiple_of(number * 64, 64)
+        here = pl.ds(pl.multiple_of(t * rows + off, 64), 64)
+        branch = total(0, off) + bo[...] + bd[...]
+        residual = T[here, :].astype(F32) + branch
+        mixed[pl.ds(off, 64), :] = residual.astype(BF16)
+        normed, inverse_root = norm_rows(t * rows + off, 64)
+        grad = total(1, off)
+        grad = inverse_root * (
+            grad
+            - jnp.mean(grad, axis=1, keepdims=True)
+            - normed * jnp.mean(grad * normed, axis=1, keepdims=True)
+        ) + upstream_rows(here).astype(F32)
+        igrad[pl.ds(off, 64), :] = grad
+        spot = lax.broadcasted_iota(jnp.int32, SQ.shape, 1)
+        for place, value in enumerate((residual, branch, grad)):
+            SQ[...] += jnp.where(spot == place, square(value), 0.0)
+
+    members = (4, ring, ring, 4, ring)
+
+    def share(stage, offset):
+        over_tensor = stage in (0, 3)
+        mate = (dp, lax.rem(t + offset, 4)) if over_tensor else (lax.rem(dp + offset, ring), t)
+        src, dst = (
+            lambda: (ES, EX.at[t]),
+            lambda: (EROWS.at[lax.rem(dp + offset, ring)], EY.at[dp]),
+            lambda: (SUMS.at[dp], SUMS.at[dp]),
+            lambda: (EQ.at[0], EZ.at[t]),
+            lambda: (EQ.at[1], EZ.at[4 + dp]),
+        )[stage]()
+        number = sum(members[:stage]) - stage + offset - 1
+        return remote(src, dst, e_s.at[number], e_r.at[number], mate)
+
+    def share_start(stage):
+        for offset in range(1, members[stage]):
+            share(stage, offset).start()
+
+    def share_wait(stage):
+        for offset in range(1, members[stage]):
+            share(stage, offset).wait_recv()
+
+    def added(ref, first, count):
+        total = ref[first]
+        for number in range(1, count):
+            total = total + ref[first + number]
+        return total
+
+    def share_tensor():
+        ES[...] = SV[...]
+        EX[t] = SV[...]
+        share_start(0)
+
+    def share_rows():
+        share_wait(0)
+        row = lax.broadcasted_iota(jnp.int32, SV.shape, 0)
+        total = jnp.where(row < 5, added(EX, 0, 4), SV[...])
+        for place in range(ring):
+            EROWS[:, place, :] = total[:, place * 128 : (place + 1) * 128]
+        EY[dp] = EROWS[dp]
+        share_start(1)
+
+    def share_gather():
+        share_wait(1)
+        SUMS[dp] = added(EY, 0, ring)
+        share_start(2)
+
+    def share_squares():
+        EQ[0] = SQ[...]
+        EZ[t] = SQ[...]
+        share_start(3)
+
+    def share_squares_dp():
+        share_wait(3)
+        total = added(EZ, 0, 4)
+        EQ[1] = total
+        EZ[4 + dp] = total
+        share_start(4)
+
+    def share_end():
+        share_wait(2)
+        share_wait(4)
+        SQO[...] = added(EZ, 4, ring)
 
     def chunk(direction, step):
         return lax.rem(at + ring - step, ring) if direction == 0 else lax.rem(at + step, ring)
@@ -632,216 +682,257 @@
     def gathered(direction, step):
         return lax.rem(at + 1 + ring - step, ring) if direction == 0 else lax.rem(at + ring - 1 + step, ring)
 
+    def left_of(segment, direction, step):
+        columns = pl.ds(pl.multiple_of(chunk(direction, step) * 128, 128), 128)
+        return (HID, FI, AI)[segment][:, columns]
+
+    def own_piece(step, part):
+        for direction in range(2):
+            PSD[lax.rem(step, PARTS), direction, :, part * 128 : (part + 1) * 128] = dot_tn(
+                left_of(0, direction, step), CB[part, direction]
+            )
+
+    def own_down(step):
+        for direction in range(2):
+            right = jnp.concatenate([CB[part, direction] for part in range(PARTS)], axis=1)
+            PSD[lax.rem(step, PARTS), direction] = dot_tn(left_of(0, direction, step), right)
+
     def own_partial(segment, step):
         for direction in range(2):
-            number = chunk(direction, step)
-            columns = pl.ds(pl.multiple_of(number * 128, 128), 128)
-            if segment < 2:
-                left, right = (HID, C) if segment == 0 else (FI, PG)
-                PSC[direction] = dot_tn(left[:, columns], right[:, direction * 512 : (direction + 1) * 512])
+            left = left_of(segment, direction, step)
+            if segment == 1:
+                PSC[direction] = dot_tn(left, PG[:, direction * 512 : (direction + 1) * 512])
             else:
-                PSC[direction, :, 0:384] = dot_tn(AI[:, columns], QG[:, direction * 384 : (direction + 1) * 384])
+                number = chunk(direction, step)
+                PSC[direction, :, 0:384] = dot_tn(left, QG[:, direction * 384 : (direction + 1) * 384])
                 PSC[direction, :, 384:512] = dot_tn(
-                    CTX[:, direction * 128 : (direction + 1) * 128], C[:, columns]
+                    CTX[:, direction * 128 : (direction + 1) * 128], CB[lax.rem(number, PARTS), lax.div(number, PARTS)]
                 )
 
-    def scatter(segment, direction, part, step):
+    def parts_of(segment, piece):
+        return pl.ds(piece * TOGETHER[segment], TOGETHER[segment])
+
+    def sems_of(segment, direction, piece, step):
+        return r_s.at[segment, direction, piece], r_r.at[segment, direction, piece, lax.rem(step, ring)]
+
+    def scatter(segment, direction, piece, step):
+        parts = parts_of(segment, piece)
         return remote(
-            RSB.at[segment, direction, part, step], RSB.at[segment, direction, part, step + 1],
-            r_s.at[segment, direction, part, step], r_r.at[segment, direction, part, step], onward[direction],
-        )
-
-    def collect(segment, direction, part, step):
-        piece = GB.at[segment, direction, part, gathered(direction, step)]
-        sem = ring - 1 + step
+            RSB.at[segment, direction, parts, step], RSB.at[segment, direction, parts, step + 1],
+            *sems_of(segment, direction, piece, step), onward[direction],
+        )
+
+    def collect(segment, direction, piece, step):
+        block = GB.at[segment, direction, parts_of(segment, piece), gathered(direction, step)]
         return remote(
-            piece, piece,
-            r_s.at[segment, direction, part, sem], r_r.at[segment, direction, part, sem], onward[direction],
-        )
-
-    pieces = [(part, direction) for part in range(PARTS) for direction in range(2)]
-
-    def ring_open(segment):
-        own_partial(segment, 0)
-        for part, direction in pieces:
-            RSB[segment, direction, part, 0] = PSC[direction, :, part * 128 : (part + 1) * 128].astype(BF16)
-            scatter(segment, direction, part, 0).start()
-
-    def ring_scatter(segment, step):
-        for part, direction in pieces:
-            scatter(segment, direction, part, step - 1).wait_recv()
-            RSB[segment, direction, part, step] = (
-                RSB[segment, direction, part, step].astype(F32)
-                + PSC[direction, :, part * 128 : (part + 1) * 128]
-            ).astype(BF16)
-            scatter(segment, direction, part, step).start()
-
-    def ring_turn(segment):
+            block, block, *sems_of(segment, direction, piece, ring - 1 + step), onward[direction]
+        )
+
+    turns = ring - 1
+
+    def during(condition, work):
+        pl.when(condition)(work)
+
+    def pieces(segment, parts=None):
+        parts = range(PARTS // TOGETHER[segment]) if parts is None else parts
+        return [(piece, direction) for piece in parts for direction in range(2)]
+
+    def members_of(segment, piece):
+        return range(piece * TOGETHER[segment], (piece + 1) * TOGETHER[segment])
+
+    def term(segment, direction, part, step):
+        columns = slice(part * 128, (part + 1) * 128)
+        if segment == 0:
+            return PSD[lax.rem(step, PARTS), direction, :, columns]
+        return PSC[direction, :, columns]
+
+    def sent(segment, direction, piece):
+        scatter(segment, direction, piece, 0).wait_send()
+
+    def ring_open(segment, parts=None):
+        for piece, direction in pieces(segment, parts):
+            for part in members_of(segment, piece):
+                RSB[segment, direction, part, 0] = term(segment, direction, part, 0).astype(BF16)
+            scatter(segment, direction, piece, 0).start()
+
+    def ring_scatter(segment, step, parts=None):
+        for piece, direction in pieces(segment, parts):
+            scatter(segment, direction, piece, step - 1).wait_recv()
+            for part in members_of(segment, piece):
+                RSB[segment, direction, part, step] = (
+                    RSB[segment, direction, part, step].astype(F32) + term(segment, direction, part, step)
+                ).astype(BF16)
+            sent(segment, direction, piece)
+            scatter(segment, direction, piece, step).start()
+
+    def ring_turn(segment, parts=None):
         last = ring - 1
-        for part, direction in pieces:
-            scatter(segment, direction, part, last - 1).wait_recv()
-            GB[segment, direction, part, gathered(direction, 0)] = (
-                RSB[segment, direction, part, last].astype(F32)
-                + PSC[direction, :, part * 128 : (part + 1) * 128]
-            ).astype(BF16)
-            collect(segment, direction, part, 0).start()
-
-    def ring_collect(segment, step):
-        for part, direction in pieces:
-            collect(segment, direction, part, step - 1).wait_recv()
-            collect(segment, direction, part, step).start()
-
-    def ring_close(segment):
-        for part, direction in pieces:
-            collect(segment, direction, part, ring - 2).wait_recv()
+        for piece, direction in pieces(segment, parts):
+            scatter(segment, direction, piece, last - 1).wait_recv()
+            for part in members_of(segment, piece):
+                GB[segment, direction, part, gathered(direction, 0)] = (
+                    RSB[segment, direction, part, last].astype(F32) + term(segment, direction, part, last)
+                ).astype(BF16)
+            sent(segment, direction, piece)
+            collect(segment, direction, piece, 0).start()
+
+    def ring_collect(segment, step, parts=None):
+        for piece, direction in pieces(segment, parts):
+            collect(segment, direction, piece, step - 1).wait_recv()
+            sent(segment, direction, piece)
+            collect(segment, direction, piece, step).start()
+
+    def ring_close(segment, parts=None):
+        for piece, direction in pieces(segment, parts):
+            collect(segment, direction, piece, ring - 2).wait_recv()
+            sent(segment, direction, piece)
+
+    def down_slot(slot):
+        @pl.when(slot <= turns)
+        def _():
+            own_down(slot)
+
+        for part in range(PARTS):
+            event = slot - part
+            during(event < PARTS, lambda: own_piece(event, part))
+            during(event < turns, lambda: ring_scatter(0, event, (part,)))
+            during(event == turns, lambda: ring_turn(0, (part,)))
+            during((event > turns) & (event < 2 * turns), lambda: ring_collect(0, event - turns, (part,)))
+            during(event == 2 * turns, lambda: ring_close(0, (part,)))
 
     for copy in local[:3]:
         copy.wait()
 
-    @pl.loop(0, 4)
+    def place_of(step):
+        return 2 * lax.rem(x + lax.div(step, 2), 2) + lax.rem(core + lax.rem(step, 2), 2)
+
+    @pl.loop(0, 8)
     def _(step):
         @pl.when(step == 1)
         def _():
-            gather(0, 0).wait_recv()
+            for copy in local[3:]:
+                copy.wait()
+            for kind in range(PARTS + 1):
+                gather(1, kind).start()
 
         @pl.when(step == 2)
         def _():
-            gather(0, 1).wait_recv()
-            gather(0, 3).start()
-            gather(0, 2).wait_recv()
-            gather(0, 4).start()
-
-        @pl.when(step == 3)
+            gather(0, 0).wait_recv()
+
+        for half in range(2):
+
+            @pl.when(step == 4 + 2 * half)
+            def _():
+                gather(0, 1 + half).wait_recv()
+                gather(0, 3 + half).start()
+
+            @pl.when(step == 5 + 2 * half)
+            def _():
+                gather(0, 3 + half).wait_recv()
+
+        late = lax.div(step, 4)
+        block = place_of(2 * late + jnp.where(late == 1, lax.rem(step, 2), lax.div(step, 2)))
+        forward_block(block, jnp.where(late == 1, lax.div(step - 4, 2), lax.rem(step, 2)))
+
+        @pl.when(step == 5)
         def _():
-            gather(0, 3).wait_recv()
-            gather(0, 4).wait_recv()
-
-        forward_block(2 * lax.rem(x + lax.div(step, 2), 2) + lax.rem(core + lax.rem(step, 2), 2))
-
-    for copy in local[3:]:
-        copy.wait()
-
-    def place_of(step):
-        return 2 * lax.rem(x + lax.div(step, 2), 2) + lax.rem(core + lax.rem(step, 2), 2)
-
-    gather(1, 1).wait_recv()
-    gather(1, 3).start()
-    cotangent_block(place_of(0))
+            cotangent_block(place_of(0))
+
     gather(1, 0).wait_recv()
-    gather(1, 2).wait_recv()
-    gather(1, 4).start()
-    gather(1, 3).wait_recv()
-    gather(1, 4).wait_recv()
-
-    turns = ring - 1
-
-    def during(condition, work):
-        pl.when(condition)(work)
-
-    ring_open(0)
-
-    @pl.loop(1, 4)
-    def _(step):
-        cotangent_block(place_of(step))
-
+    for slot in range(PARTS):
+        gather(1, 1 + slot).wait_recv()
+        gather(1, 1 + PARTS + slot).start()
+        for part in range(slot):
+            own_piece(slot - part, part)
+            ring_scatter(0, slot - part, (part,))
+        gather(1, 1 + PARTS + slot).wait_recv()
+        own_piece(0, slot)
+        ring_open(0, (slot,))
+        if slot == 0:
+            cotangent_block(place_of(1))
+
+    cotangent_block(place_of(2))
+    down_slot(4)
+    cotangent_block(place_of(3))
+    own_partial(1, 0)
     ring_open(1)
 
-    @pl.loop(1, turns)
-    def _(step):
-        for segment in range(2):
+    def advance(segment, step):
+        @pl.when(step <= turns)
+        def _():
             own_partial(segment, step)
-            ring_scatter(segment, step)
-
-        @pl.loop(2 * step - 2, 2 * step)
-        def _(unit):
-            attention_unit(unit)
-
-    for segment in range(2):
-        own_partial(segment, turns)
-        ring_turn(segment)
-
-    @pl.loop(1, 3)
-    def _(step):
-        @pl.loop(2 * step + 10, 2 * step + 12)
-        def _(unit):
-            attention_unit(unit)
-
-        for segment in range(2):
-            ring_collect(segment, step)
+
+        during(step < turns, lambda: ring_scatter(segment, step))
+        during(step == turns, lambda: ring_turn(segment))
+        during(step > turns, lambda: ring_collect(segment, step - turns))
+
+    @pl.loop(0, heads * blocks)
+    def _(unit):
+        slot = 5 + lax.div(unit, 2)
+        during(lax.rem(unit, 2) == 0, lambda: down_slot(slot))
+        during(lax.rem(unit, 2) == 1, lambda: advance(1, slot - 4))
+        attention_unit(unit)
 
     @pl.loop(0, blocks)
     def _(block):
+        during(block == 0, lambda: down_slot(13))
+        during(block == 2, lambda: ring_collect(1, 2))
         assemble(block)
 
+    own_partial(2, 0)
     ring_open(2)
-
-    @pl.loop(3, turns)
-    def _(step):
-        for segment in range(2):
-            ring_collect(segment, step)
-        own_partial(2, step - 2)
-        ring_scatter(2, step - 2)
-
-        @pl.when(step <= 4)
+    SV[4:5, :] = jnp.sum(upstream_rows(pl.ds(t * rows, rows)).astype(F32), axis=0, keepdims=True)
+
+    @pl.loop(0, 8)
+    def _(half):
+        slot = 14 + lax.div(half, 2)
+        during(half == 2, lambda: chip_sum(0))
+        during(half == 4, lambda: chip_sum(1))
+        during(half == 5, share_tensor)
+        during(lax.rem(half, 2) == 0, lambda: down_slot(slot))
+
+        @pl.when(lax.rem(half, 2) == 1)
         def _():
-            @pl.loop(2 * step - 6, 2 * step - 4)
+            ring_collect(1, slot - 11)
+            own_partial(2, slot - 13)
+            ring_scatter(2, slot - 13)
+
+        @pl.when(half < 2)
+        def _():
+            @pl.loop(2 * half, 2 * half + 2)
+            def _(number):
+                branch_block(number)
+
+        @pl.when((half >= 2) & (half < 4))
+        def _():
+            @pl.loop(2 * half - 4, 2 * half - 2)
             def _(number):
                 back_block(number)
 
-        @pl.when(step == 5)
-        def _():
-            @pl.loop(0, 4)
-            def _(number):
-                branch_block(number)
-
-            chip_sum(1)
-
-        during(step == 6, lambda: chip_sum(0))
-
-    for segment in range(2):
-        ring_close(segment)
-
-    @pl.loop(5, turns)
+    ring_close(1)
+
+    @pl.loop(5, 2 * turns)
     def _(step):
-        own_partial(2, step)
-        ring_scatter(2, step)
-
-    own_partial(2, turns)
-    ring_turn(2)
-
-    @pl.loop(1, turns)
-    def _(step):
-        ring_collect(2, step)
-
-        @pl.when(step == 3)
-        def _():
-            finish()
-            share_send(0)
-
-        @pl.when(step == 5)
-        def _():
-            share_receive(0)
-            share_send(1)
+        advance(2, step)
+        during(step == 6, finish_start)
+        during((step >= 6) & (step < 10), lambda: finish_part(step - 6))
+        during(step == 7, share_rows)
+        during(step == 10, share_gather)
+        during(step == 9, share_squares)
+        during(step == 11, share_squares_dp)
 
     ring_close(2)
-    share_receive(1)
+    share_end()
 
     for which in range(2):
-        for kind in range(5):
+        for kind in range(kinds[which]):
             gather(which, kind).wait_send()
         for slot in range(2):
             to_core(which, slot).wait_send()
         to_x(which).wait_send()
-    for over in range(2):
-        for offset in range(1, members[over]):
-            share(over, offset).wait_send()
-    for segment in range(3):
-
-        @pl.loop(0, ring - 1)
-        def _(step):
-            for part, direction in pieces:
-                scatter(segment, direction, part, step).wait_send()
-                collect(segment, direction, part, step).wait_send()
+    for stage in range(5):
+        for offset in range(1, members[stage]):
+            share(stage, offset).wait_send()
 
 
 def angle_parts(seq_len):
@@ -870,7 +961,7 @@
     V = pltpu.VMEM
     D = pltpu.SemaphoreType.DMA
     scratch = [
-        V((seq, width), BF16), V((seq, width), BF16), V((seq, width), BF16), V((seq, width), BF16),
+        V((seq, width), BF16), V((PARTS, 2, seq, 128), BF16), V((seq, width), BF16), V((seq, width), BF16),
         V((seq, hidden_width), BF16), V((seq, hidden_width), F32), V((seq, hidden_width), BF16),
         V((seq, qkv_width), BF16),
         V((heads, seq, HD), BF16), V((heads, seq, HD), BF16), V((heads, seq, HD), BF16),
@@ -878,23 +969,26 @@
         V((heads, seq, HD), F32), V((heads, HD, seq), F32), V((heads, HD, seq), F32),
         V((seq, 128), F32), V((seq, 128), F32),
         V(qkv_weight.shape, BF16), V(out_weight.shape, BF16), V(up_weight.shape, BF16), V(down_weight.shape, BF16),
-        V((3, 2, PARTS, ring, 128, 128), BF16), V((2, 128, 512), F32),
+        V((3, 2, PARTS, ring, 128, 128), BF16), V((PARTS, 2, 128, 512), F32), V((2, 128, 512), F32),
         V((2, seq, width), BF16), V((2, 2, rows, width), BF16), V((2, rows, width), BF16),
-        V((2, 8, width), F32), V((4 + ring, 8, width), F32),
-        D((6,)), D((2, 5)), D((2, 5)),
-        D((3, 2, PARTS, 2 * ring - 2)), D((3, 2, PARTS, 2 * ring - 2)),
-        D((2, 3)), D((2, 3)), D((2, ring)), D((2, ring)),
+        V((8, width), F32), V((8, width), F32), V((4, 8, width), F32),
+        V((ring, 8, 128), F32), V((ring, 8, 128), F32), V((8, 128), F32),
+        V((2, 8, 128), F32), V((4 + ring, 8, 128), F32),
+        D((6 + 2 * PARTS,)), D((2, 1 + 2 * PARTS)), D((2, 1 + 2 * PARTS)),
+        D((3, 2, PARTS)), D((3, 2, PARTS, ring)),
+        D((2, 3)), D((2, 3)), D((3 * ring + 3,)), D((3 * ring + 3,)),
     ]
-    mixed, input_grad, gradients, sums = pl.pallas_call(
+    mixed, input_grad, gradients, sums, squares = pl.pallas_call(
         functools.partial(fused_kernel, ring),
         out_shape=[
             V((rows, width), BF16),
             V((rows, width), F32),
             V((3, 2, PARTS, ring, 128, 128), BF16),
-            V((8, width), F32),
+            V((ring, 8, 128), F32),
+            V((8, 128), F32),
         ],
         in_specs=[hbm, hbm] + [vmem] * 8 + [hbm] * 4 + [vmem] * 4,
-        out_specs=[vmem] * 4,
+        out_specs=[vmem] * 5,
         scratch_shapes=scratch,
         compiler_params=pltpu.CompilerParams(
             collective_id=0, has_side_effects=True, vmem_limit_bytes=VMEM_LIMIT
@@ -907,12 +1001,14 @@
         qkv_weight, out_weight, up_weight, down_weight, cos_a, sin_a, cos_b, sin_b,
     )
     elements = rows * width * ring * lax.axis_size("tensor")
-    return closing(mixed, input_grad, gradients, sums, elements, down_weight, up_weight, qkv_weight, out_weight)
+    return closing(
+        mixed, input_grad, gradients, sums, squares, elements, down_weight, up_weight, qkv_weight, out_weight
+    )
 
 
 def closing_kernel(
     elements,
-    mixed, igrad, GB, SV,
+    mixed, igrad, GB, SUMS, SQUARES,
     mixed_o, igrad_o, ga_o, ba_o, gm_o, bm_o, gq_o, bqkv_o, go_o, bo_o, gu_o, bup_o, gd_o, bd_o, stats_o,
     SD, SU, SQ, SO, sems, msem,
 ):
@@ -941,28 +1037,28 @@
             copies.append(copy)
     copies.append(pltpu.make_async_copy(SO, go_o, msem.at[2]))
     copies[-1].start()
-    for row, out in enumerate((ga_o, ba_o, gm_o, bm_o, bo_o)):
-        out[...] = SV[row : row + 1, :]
-    bd_o[...] = SV[4:5, :]
-    bup_o[...] = SV[6:7, :]
-    bqkv_o[...] = SV[7, : bqkv_o.shape[0]]
-    stats_o[...] = jnp.sqrt(SV[5, : stats_o.shape[0]] * (1.0 / elements))
+    for row, out in ((0, ga_o), (1, ba_o), (2, gm_o), (3, bm_o), (4, bo_o), (4, bd_o), (6, bup_o)):
+        for place in range(SUMS.shape[1]):
+            out[:, place * 128 : (place + 1) * 128] = SUMS[row, place : place + 1, :]
+    for place in range(bqkv_o.shape[0] // 128):
+        bqkv_o[place * 128 : (place + 1) * 128] = SUMS[7, place, :]
+    stats_o[...] = jnp.sqrt(SQUARES[0, : stats_o.shape[0]] * (1.0 / elements))
     for copy in copies:
         copy.wait()
 
 
-def closing(mixed, input_grad, gradients, sums, elements, down_weight, up_weight, qkv_weight, out_weight):
+def closing(mixed, input_grad, gradients, sums, squares, elements, down_weight, up_weight, qkv_weight, out_weight):
     hbm = pl.BlockSpec(memory_space=pl.ANY)
     vmem = pl.BlockSpec(memory_space=pltpu.VMEM)
 
     def like(array, dtype=F32):
         return jax.ShapeDtypeStruct(array.shape, dtype)
 
-    width = sums.shape[1]
+    width = mixed.shape[1]
     row = jax.ShapeDtypeStruct((1, width), F32)
     outs = pl.pallas_call(
         functools.partial(closing_kernel, elements),
-        in_specs=[vmem] * 4,
+        in_specs=[vmem] * 5,
         out_specs=[
             hbm, hbm, vmem, vmem, vmem, vmem, hbm, vmem, hbm, vmem, hbm, vmem, hbm, vmem, vmem,
         ],
@@ -981,7 +1077,7 @@
         ],
         compiler_params=pltpu.CompilerParams(vmem_limit_bytes=24 << 20),
         name="outputs",
-    )(mixed, input_grad, gradients, sums)
+    )(mixed, input_grad, gradients, sums, squares)
     return tuple(out.reshape(-1) if out.shape == (1, width) else out for out in outs)
 
 

time: 174 us -> 164 us (0.943)
  Pallas kernels: 173 us -> 163 us
    pallas_call x1, Pallas kernels: 167 us -> 157 us  [per_device_fused(): pl.pallas_call(functools.partial(fused_kernel, ring), out_shape=[V((rows,...]
where the time goes in v4:
time: 164 us
  Pallas kernels  163 us (99%)
    pallas_call x1, Pallas kernels, per_device_fused(): pl.pallas_call(functools.partial(fused_kernel, ring), out_shape=[V((rows,...  157 us
    pallas_call x1, Pallas kernels, closing(): pl.pallas_call(functools.partial(closing_kernel, elements), in_specs=[vme...  5.95 us

profile of v4, /device:TPU:0, one launch (start us, length us, event | category | flops | bytes accessed | tf_op | source)
XLA Modules:
  0.0 164.1 jit_solution(10961201402965709361)
XLA Ops:
  0.7 157.3 %layer.1 = (bf16[256,1024]{1,0:T(8,128)(2,1)S(1)}, f32[256,1024]{1,0:T(8,128)S(1)}, bf16[3,2,4,8,128,128]{5,4,3,2,1,0:T(8,128)(2,1)S(1)}, f32[8,8,128]{2,1,0:T(8,128)S(1)}, f32[8,128]{1,0:T(8,128)S(1)}) custom-call(bf16[256,1024]{1,0:T(8,128)(2,1)} %tok.1, bf16[256,1024]{1,0:T(8,128)(2,1)} %cot.1, f32[1,1024]{1,0:T(1,128)} %bitcast.14, f32[1,1024]{1,0:T(1,128)} %bitcast.15, ...), custom_call_target="tpu_custom_call" | custom-call | tf_op jit(solution)/shard_map/layer/pallas_call | solution.py:981
  158.0 5.9 %outputs.1 = (bf16[256,1024]{1,0:T(8,128)(2,1)}, f32[256,1024]{1,0:T(8,128)}, f32[1,1024]{1,0:T(1,128)}, f32[1,1024]{1,0:T(1,128)}, f32[1,1024]{1,0:T(1,128)}, /...) custom-call(bf16[256,1024]{1,0:T(8,128)(2,1)S(1)} %get-tuple-element, ...), custom_call_target="tpu_custom_call" | custom-call | tf_op jit(solution)/shard_map/outputs/pallas_call | solution.py:1059

commit v5 on v4

--- a/solution.py
+++ b/solution.py
@@ -269,7 +269,12 @@
 MESH = pl.DeviceIdType.MESH
 TILE = 256
 PARTS = 4
-TOGETHER = (1, 2, 1)
+TOGETHER = (1, 4, 1)
+SPLIT = (1, 1, 1)
+
+
+def ring_pieces(segments):
+    return sum(2 * (PARTS // TOGETHER[number] * SPLIT[number]) for number in range(segments))
 
 
 def dot_nn(left, right):
@@ -326,7 +331,7 @@
         )
 
     def gather(which, kind):
-        sems = (g_s.at[which, kind], g_r.at[which, kind])
+        sems = (g_s.at[5 * which + kind], g_r.at[5 * which + kind])
         own = pl.ds(t * rows, rows)
         there = pl.ds(x_block * rows, rows)
         if which == 1:
@@ -585,28 +590,28 @@
             to_x(which).wait_recv()
     def total(which, off):
         return (
-            PART[which, pl.ds(pl.multiple_of(t * rows + off, 64), 64), :].astype(F32)
-            + RA[which, 0, pl.ds(off, 64), :].astype(F32)
-            + RB[which, pl.ds(off, 64), :].astype(F32)
+            PART[which, pl.ds(pl.multiple_of(t * rows + off, 32), 32), :].astype(F32)
+            + RA[which, 0, pl.ds(off, 32), :].astype(F32)
+            + RB[which, pl.ds(off, 32), :].astype(F32)
         )
 
     def square(value):
         return jnp.sum(jnp.sum(value * value, axis=1, keepdims=True), axis=0, keepdims=True)
 
     def finish_part(number):
-        off = pl.multiple_of(number * 64, 64)
-        here = pl.ds(pl.multiple_of(t * rows + off, 64), 64)
+        off = pl.multiple_of(number * 32, 32)
+        here = pl.ds(pl.multiple_of(t * rows + off, 32), 32)
         branch = total(0, off) + bo[...] + bd[...]
         residual = T[here, :].astype(F32) + branch
-        mixed[pl.ds(off, 64), :] = residual.astype(BF16)
-        normed, inverse_root = norm_rows(t * rows + off, 64)
+        mixed[pl.ds(off, 32), :] = residual.astype(BF16)
+        normed, inverse_root = norm_rows(t * rows + off, 32)
         grad = total(1, off)
         grad = inverse_root * (
             grad
             - jnp.mean(grad, axis=1, keepdims=True)
             - normed * jnp.mean(grad * normed, axis=1, keepdims=True)
         ) + upstream_rows(here).astype(F32)
-        igrad[pl.ds(off, 64), :] = grad
+        igrad[pl.ds(off, 32), :] = grad
         spot = lax.broadcasted_iota(jnp.int32, SQ.shape, 1)
         for place, value in enumerate((residual, branch, grad)):
             SQ[...] += jnp.where(spot == place, square(value), 0.0)
@@ -623,16 +628,19 @@
             lambda: (EQ.at[0], EZ.at[t]),
             lambda: (EQ.at[1], EZ.at[4 + dp]),
         )[stage]()
-        number = sum(members[:stage]) - stage + offset - 1
-        return remote(src, dst, e_s.at[number], e_r.at[number], mate)
+        return remote(src, dst, e_s.at[stage], e_r.at[stage], mate)
 
     def share_start(stage):
         for offset in range(1, members[stage]):
             share(stage, offset).start()
 
+    def share_all(stage):
+        ref, first = ((EX, 0), (EY, 0), (SUMS, 0), (EZ, 0), (EZ, 4))[stage]
+        whole = ref.at[pl.ds(first, members[stage] - 1)]
+        return remote(whole, whole, e_s.at[stage], e_r.at[stage], core_mate)
+
     def share_wait(stage):
-        for offset in range(1, members[stage]):
-            share(stage, offset).wait_recv()
+        share_all(stage).wait_recv()
 
     def added(ref, first, count):
         total = ref[first]
@@ -710,20 +718,25 @@
                 )
 
     def parts_of(segment, piece):
-        return pl.ds(piece * TOGETHER[segment], TOGETHER[segment])
+        return pl.ds(piece // SPLIT[segment] * TOGETHER[segment], TOGETHER[segment])
+
+    def rows_of(segment, piece):
+        count = 128 // SPLIT[segment]
+        return slice(piece % SPLIT[segment] * count, (piece % SPLIT[segment] + 1) * count)
 
     def sems_of(segment, direction, piece, step):
-        return r_s.at[segment, direction, piece], r_r.at[segment, direction, piece, lax.rem(step, ring)]
+        number = ring_pieces(segment) + direction * (PARTS // TOGETHER[segment] * SPLIT[segment]) + piece
+        return r_s.at[number], r_r.at[number * ring + lax.rem(step, ring)]
 
     def scatter(segment, direction, piece, step):
-        parts = parts_of(segment, piece)
+        parts, here = parts_of(segment, piece), rows_of(segment, piece)
         return remote(
-            RSB.at[segment, direction, parts, step], RSB.at[segment, direction, parts, step + 1],
+            RSB.at[segment, direction, parts, step, here], RSB.at[segment, direction, parts, step + 1, here],
             *sems_of(segment, direction, piece, step), onward[direction],
         )
 
     def collect(segment, direction, piece, step):
-        block = GB.at[segment, direction, parts_of(segment, piece), gathered(direction, step)]
+        block = GB.at[segment, direction, parts_of(segment, piece), gathered(direction, step), rows_of(segment, piece)]
         return remote(
             block, block, *sems_of(segment, direction, piece, ring - 1 + step), onward[direction]
         )
@@ -734,33 +747,36 @@
         pl.when(condition)(work)
 
     def pieces(segment, parts=None):
-        parts = range(PARTS // TOGETHER[segment]) if parts is None else parts
+        parts = range(PARTS // TOGETHER[segment] * SPLIT[segment]) if parts is None else parts
         return [(piece, direction) for piece in parts for direction in range(2)]
 
     def members_of(segment, piece):
-        return range(piece * TOGETHER[segment], (piece + 1) * TOGETHER[segment])
-
-    def term(segment, direction, part, step):
+        first = piece // SPLIT[segment] * TOGETHER[segment]
+        return range(first, first + TOGETHER[segment])
+
+    def term(segment, direction, part, step, here):
         columns = slice(part * 128, (part + 1) * 128)
         if segment == 0:
-            return PSD[lax.rem(step, PARTS), direction, :, columns]
-        return PSC[direction, :, columns]
+            return PSD[lax.rem(step, PARTS), direction, here, columns]
+        return PSC[direction, here, columns]
 
     def sent(segment, direction, piece):
         scatter(segment, direction, piece, 0).wait_send()
 
     def ring_open(segment, parts=None):
         for piece, direction in pieces(segment, parts):
+            here = rows_of(segment, piece)
             for part in members_of(segment, piece):
-                RSB[segment, direction, part, 0] = term(segment, direction, part, 0).astype(BF16)
+                RSB[segment, direction, part, 0, here] = term(segment, direction, part, 0, here).astype(BF16)
             scatter(segment, direction, piece, 0).start()
 
     def ring_scatter(segment, step, parts=None):
         for piece, direction in pieces(segment, parts):
+            here = rows_of(segment, piece)
             scatter(segment, direction, piece, step - 1).wait_recv()
             for part in members_of(segment, piece):
-                RSB[segment, direction, part, step] = (
-                    RSB[segment, direction, part, step].astype(F32) + term(segment, direction, part, step)
+                RSB[segment, direction, part, step, here] = (
+                    RSB[segment, direction, part, step, here].astype(F32) + term(segment, direction, part, step, here)
                 ).astype(BF16)
             sent(segment, direction, piece)
             scatter(segment, direction, piece, step).start()
@@ -768,10 +784,11 @@
     def ring_turn(segment, parts=None):
         last = ring - 1
         for piece, direction in pieces(segment, parts):
+            here = rows_of(segment, piece)
             scatter(segment, direction, piece, last - 1).wait_recv()
             for part in members_of(segment, piece):
-                GB[segment, direction, part, gathered(direction, 0)] = (
-                    RSB[segment, direction, part, last].astype(F32) + term(segment, direction, part, last)
+                GB[segment, direction, part, gathered(direction, 0), here] = (
+                    RSB[segment, direction, part, last, here].astype(F32) + term(segment, direction, part, last, here)
                 ).astype(BF16)
             sent(segment, direction, piece)
             collect(segment, direction, piece, 0).start()
@@ -787,18 +804,20 @@
             collect(segment, direction, piece, ring - 2).wait_recv()
             sent(segment, direction, piece)
 
-    def down_slot(slot):
-        @pl.when(slot <= turns)
-        def _():
-            own_down(slot)
-
+    def down_terms(slot):
+        during((slot >= PARTS) & (slot <= turns), lambda: own_down(slot))
         for part in range(PARTS):
             event = slot - part
-            during(event < PARTS, lambda: own_piece(event, part))
+            during((event > 0) & (event < PARTS), lambda: own_piece(event, part))
+
+    def down_slot(slot):
+        for part in range(PARTS):
+            event = slot - part
             during(event < turns, lambda: ring_scatter(0, event, (part,)))
             during(event == turns, lambda: ring_turn(0, (part,)))
             during((event > turns) & (event < 2 * turns), lambda: ring_collect(0, event - turns, (part,)))
             during(event == 2 * turns, lambda: ring_close(0, (part,)))
+        down_terms(slot + 1)
 
     for copy in local[:3]:
         copy.wait()
@@ -843,11 +862,15 @@
         gather(1, 1 + slot).wait_recv()
         gather(1, 1 + PARTS + slot).start()
         for part in range(slot):
-            own_piece(slot - part, part)
             ring_scatter(0, slot - part, (part,))
         gather(1, 1 + PARTS + slot).wait_recv()
         own_piece(0, slot)
         ring_open(0, (slot,))
+        if slot == PARTS - 1:
+            down_terms(PARTS)
+        else:
+            for part in range(slot + 1):
+                own_piece(slot + 1 - part, part)
         if slot == 0:
             cotangent_block(place_of(1))
 
@@ -866,26 +889,32 @@
         during(step == turns, lambda: ring_turn(segment))
         during(step > turns, lambda: ring_collect(segment, step - turns))
 
-    @pl.loop(0, heads * blocks)
-    def _(unit):
-        slot = 5 + lax.div(unit, 2)
-        during(lax.rem(unit, 2) == 0, lambda: down_slot(slot))
-        during(lax.rem(unit, 2) == 1, lambda: advance(1, slot - 4))
-        attention_unit(unit)
+    units = heads * blocks
+
+    @pl.loop(0, 12)
+    def _(half):
+        slot = 5 + lax.div(half, 2)
+        during(lax.rem(half, 2) == 0, lambda: down_slot(slot))
+        during(lax.rem(half, 2) == 1, lambda: advance(1, slot - 4))
+        first = 3 * lax.div(half, 2) + 2 * lax.rem(half, 2)
+
+        @pl.loop(jnp.minimum(first, units), jnp.minimum(first + 2 - lax.rem(half, 2), units))
+        def _(unit):
+            attention_unit(unit)
 
     @pl.loop(0, blocks)
     def _(block):
-        during(block == 0, lambda: down_slot(13))
-        during(block == 2, lambda: ring_collect(1, 2))
+        during(block == 0, lambda: down_slot(11))
+        during(block == 2, lambda: advance(1, turns))
         assemble(block)
 
     own_partial(2, 0)
     ring_open(2)
     SV[4:5, :] = jnp.sum(upstream_rows(pl.ds(t * rows, rows)).astype(F32), axis=0, keepdims=True)
 
-    @pl.loop(0, 8)
+    @pl.loop(0, 12)
     def _(half):
-        slot = 14 + lax.div(half, 2)
+        slot = 12 + lax.div(half, 2)
         during(half == 2, lambda: chip_sum(0))
         during(half == 4, lambda: chip_sum(1))
         during(half == 5, share_tensor)
@@ -894,8 +923,8 @@
         @pl.when(lax.rem(half, 2) == 1)
         def _():
             ring_collect(1, slot - 11)
-            own_partial(2, slot - 13)
-            ring_scatter(2, slot - 13)
+            own_partial(2, slot - 11)
+            ring_scatter(2, slot - 11)
 
         @pl.when(half < 2)
         def _():
@@ -909,16 +938,31 @@
             def _(number):
                 back_block(number)
 
+        during(half == 8, finish_start)
+
+        @pl.when(half >= 8)
+        def _():
+            @pl.loop(2 * half - 16, 2 * half - 14)
+            def _(number):
+                finish_part(number)
+
     ring_close(1)
 
-    @pl.loop(5, 2 * turns)
+    def advance_last(step, parts):
+        during(step == turns, lambda: ring_turn(2, parts))
+        during(step > turns, lambda: ring_collect(2, step - turns, parts))
+
+    own_partial(2, turns)
+
+    @pl.loop(turns, 2 * turns)
     def _(step):
-        advance(2, step)
-        during(step == 6, finish_start)
-        during((step >= 6) & (step < 10), lambda: finish_part(step - 6))
+        for side in range(2):
+            count = PARTS * SPLIT[2] // 2
+            advance_last(step, range(side * count, (side + 1) * count))
+
         during(step == 7, share_rows)
         during(step == 10, share_gather)
-        during(step == 9, share_squares)
+        during(step == 8, share_squares)
         during(step == 11, share_squares_dp)
 
     ring_close(2)
@@ -931,8 +975,7 @@
             to_core(which, slot).wait_send()
         to_x(which).wait_send()
     for stage in range(5):
-        for offset in range(1, members[stage]):
-            share(stage, offset).wait_send()
+        share_all(stage).wait_send()
 
 
 def angle_parts(seq_len):
@@ -974,9 +1017,9 @@
         V((8, width), F32), V((8, width), F32), V((4, 8, width), F32),
         V((ring, 8, 128), F32), V((ring, 8, 128), F32), V((8, 128), F32),
         V((2, 8, 128), F32), V((4 + ring, 8, 128), F32),
-        D((6 + 2 * PARTS,)), D((2, 1 + 2 * PARTS)), D((2, 1 + 2 * PARTS)),
-        D((3, 2, PARTS)), D((3, 2, PARTS, ring)),
-        D((2, 3)), D((2, 3)), D((3 * ring + 3,)), D((3 * ring + 3,)),
+        D((6 + 2 * PARTS,)), D((6 + 2 * PARTS,)), D((6 + 2 * PARTS,)),
+        D((ring_pieces(3),)), D((ring_pieces(3) * ring,)),
+        D((2, 3)), D((2, 3)), D((5,)), D((5,)),
     ]
     mixed, input_grad, gradients, sums, squares = pl.pallas_call(
         functools.partial(fused_kernel, ring),

time: 164 us -> 163 us (level)
  no operation moved by 1% of the time
where the time goes in v5:
time: 163 us
  Pallas kernels  162 us (99%)
    pallas_call x1, Pallas kernels, per_device_fused(): pl.pallas_call(functools.partial(fused_kernel, ring), out_shape=[V((rows,...  156 us
    pallas_call x1, Pallas kernels, closing(): pl.pallas_call(functools.partial(closing_kernel, elements), in_specs=[vme...  5.95 us

profile of v5, /device:TPU:0, one launch (start us, length us, event | category | flops | bytes accessed | tf_op | source)
XLA Modules:
  0.0 162.8 jit_solution(17416870588751894578)
XLA Ops:
  0.7 156.0 %layer.1 = (bf16[256,1024]{1,0:T(8,128)(2,1)S(1)}, f32[256,1024]{1,0:T(8,128)S(1)}, bf16[3,2,4,8,128,128]{5,4,3,2,1,0:T(8,128)(2,1)S(1)}, f32[8,8,128]{2,1,0:T(8,128)S(1)}, f32[8,128]{1,0:T(8,128)S(1)}) custom-call(bf16[256,1024]{1,0:T(8,128)(2,1)} %tok.1, bf16[256,1024]{1,0:T(8,128)(2,1)} %cot.1, f32[1,1024]{1,0:T(1,128)} %bitcast.14, f32[1,1024]{1,0:T(1,128)} %bitcast.15, ...), custom_call_target="tpu_custom_call" | custom-call | tf_op jit(solution)/shard_map/layer/pallas_call | solution.py:1024
  156.7 5.9 %outputs.1 = (bf16[256,1024]{1,0:T(8,128)(2,1)}, f32[256,1024]{1,0:T(8,128)}, f32[1,1024]{1,0:T(1,128)}, f32[1,1024]{1,0:T(1,128)}, f32[1,1024]{1,0:T(1,128)}, /...) custom-call(bf16[256,1024]{1,0:T(8,128)(2,1)S(1)} %get-tuple-element, ...), custom_call_target="tpu_custom_call" | custom-call | tf_op jit(solution)/shard_map/outputs/pallas_call | solution.py:1102

commit v6 on v5

--- a/solution.py
+++ b/solution.py
@@ -864,7 +864,9 @@
         for part in range(slot):
             ring_scatter(0, slot - part, (part,))
         gather(1, 1 + PARTS + slot).wait_recv()
-        own_piece(0, slot)
+        both = dot_tn(left_of(0, 0, 0), jnp.concatenate([CB[slot, 0], CB[slot, 1]], axis=1))
+        for direction in range(2):
+            PSD[0, direction, :, slot * 128 : (slot + 1) * 128] = both[:, direction * 128 : (direction + 1) * 128]
         ring_open(0, (slot,))
         if slot == PARTS - 1:
             down_terms(PARTS)

time: 163 us -> 163 us (level)
  no operation moved by 1% of the time
where the time goes in v6:
time: 163 us; the launch traced here: 162 us
  Pallas kernels  162 us (99%)
    pallas_call x1, Pallas kernels, per_device_fused(): pl.pallas_call(functools.partial(fused_kernel, ring), out_shape=[V((rows,...  156 us
    pallas_call x1, Pallas kernels, closing(): pl.pallas_call(functools.partial(closing_kernel, elements), in_specs=[vme...  5.95 us

profile of v6, /device:TPU:0, one launch (start us, length us, event | category | flops | bytes accessed | tf_op | source)
XLA Modules:
  0.0 162.4 jit_solution(12569062621954579437)
XLA Ops:
  0.7 155.6 %layer.1 = (bf16[256,1024]{1,0:T(8,128)(2,1)S(1)}, f32[256,1024]{1,0:T(8,128)S(1)}, bf16[3,2,4,8,128,128]{5,4,3,2,1,0:T(8,128)(2,1)S(1)}, f32[8,8,128]{2,1,0:T(8,128)S(1)}, f32[8,128]{1,0:T(8,128)S(1)}) custom-call(bf16[256,1024]{1,0:T(8,128)(2,1)} %tok.1, bf16[256,1024]{1,0:T(8,128)(2,1)} %cot.1, f32[1,1024]{1,0:T(1,128)} %bitcast.14, f32[1,1024]{1,0:T(1,128)} %bitcast.15, ...), custom_call_target="tpu_custom_call" | custom-call | tf_op jit(solution)/shard_map/layer/pallas_call | solution.py:1026
  156.2 5.9 %outputs.1 = (bf16[256,1024]{1,0:T(8,128)(2,1)}, f32[256,1024]{1,0:T(8,128)}, f32[1,1024]{1,0:T(1,128)}, f32[1,1024]{1,0:T(1,128)}, f32[1,1024]{1,0:T(1,128)}, /...) custom-call(bf16[256,1024]{1,0:T(8,128)(2,1)S(1)} %get-tuple-element, ...), custom_call_target="tpu_custom_call" | custom-call | tf_op jit(solution)/shard_map/outputs/pallas_call | solution.py:1104

commit v7 on v6

--- a/solution.py
+++ b/solution.py
@@ -370,11 +370,11 @@
         pltpu.make_async_copy(wdn_h, WDN, lsem.at[4]),
         pltpu.make_async_copy(wout_h, WOUT, lsem.at[5]),
     ]
-    for copy in local:
-        copy.start()
     barrier = pltpu.get_barrier_semaphore()
     for mate in (core_mate, x_mate, following, previous):
         pl.semaphore_signal(barrier, inc=1, device_id=mate, device_id_type=MESH)
+    for copy in local:
+        copy.start()
     pl.semaphore_wait(barrier, 4)
     gather(0, 1).start()
     gather(0, 2).start()

time: 163 us -> 162 us (level)
  no operation moved by 1% of the time
where the time goes in v7:
time: 162 us
  Pallas kernels  161 us (99%)
    pallas_call x1, Pallas kernels, per_device_fused(): pl.pallas_call(functools.partial(fused_kernel, ring), out_shape=[V((rows,...  155 us
    pallas_call x1, Pallas kernels, closing(): pl.pallas_call(functools.partial(closing_kernel, elements), in_specs=[vme...  5.95 us

profile of v7, /device:TPU:0, one launch (start us, length us, event | category | flops | bytes accessed | tf_op | source)
XLA Modules:
  0.0 162.2 jit_solution(1098323912189089273)
XLA Ops:
  0.7 155.4 %layer.1 = (bf16[256,1024]{1,0:T(8,128)(2,1)S(1)}, f32[256,1024]{1,0:T(8,128)S(1)}, bf16[3,2,4,8,128,128]{5,4,3,2,1,0:T(8,128)(2,1)S(1)}, f32[8,8,128]{2,1,0:T(8,128)S(1)}, f32[8,128]{1,0:T(8,128)S(1)}) custom-call(bf16[256,1024]{1,0:T(8,128)(2,1)} %tok.1, bf16[256,1024]{1,0:T(8,128)(2,1)} %cot.1, f32[1,1024]{1,0:T(1,128)} %bitcast.14, f32[1,1024]{1,0:T(1,128)} %bitcast.15, ...), custom_call_target="tpu_custom_call" | custom-call | tf_op jit(solution)/shard_map/layer/pallas_call | solution.py:1026
  156.1 5.9 %outputs.1 = (bf16[256,1024]{1,0:T(8,128)(2,1)}, f32[256,1024]{1,0:T(8,128)}, f32[1,1024]{1,0:T(1,128)}, f32[1,1024]{1,0:T(1,128)}, f32[1,1024]{1,0:T(1,128)}, /...) custom-call(bf16[256,1024]{1,0:T(8,128)(2,1)S(1)} %get-tuple-element, ...), custom_call_target="tpu_custom_call" | custom-call | tf_op jit(solution)/shard_map/outputs/pallas_call | solution.py:1104
